TPU v7x, 256 devices: a whole 4x4x8 slice. The times are simulated.
256 devices in a mesh: region: 4 (over y_hi, core), block: 64 (over y_lo, z, x).
Axes of the slice: x: 4, y: 4 (y_hi: 2, y_lo: 2; y = y_hi * 2 + y_lo), z: 8, core: 2. Of those that a mesh axis runs over, the one named last changes fastest.
Arguments:
- features: bfloat16 [196608, 128], P(('region', 'block')), may hold values from -6 to 6
- grad_out: bfloat16 [196608, 128], P(('region', 'block')), may hold values from -6 to 6
- w1: bfloat16 [27, 128, 128], replicated, may hold values from -0.109375 to 0.109375
- w2: bfloat16 [27, 128, 128], replicated, may hold values from -0.109375 to 0.109375
- rulebook: int32 [27, 196608], P(None, ('region', 'block')), may hold values from 0 to 1024, as said below
- live_blocks: int32 [1536], P(('region', 'block')), may hold values from 0 to 1, as said below
Outputs:
- grad_in: bfloat16 [196608, 128], P(('region', 'block'))
- grad_w1: float32 [27, 128, 128], replicated
- grad_w2: float32 [27, 128, 128], replicated
Inputs may be any that keep to these rules, and one draw needn't show every extreme that they name: `rulebook`: Every entry of a padded row has that value; no entry points at a padded row or at a missing neighbour; offset 27 // 2 of a live row points at the row itself. An entry of row v of slab s other than 1024 lies between v - s * 768 and v - s * 768 + 2 * 128. `live_blocks`: the first 1 and the last 1 block of every slab are live; the padded blocks of a slab lie between them. Some slab has all 6 blocks live and some slab only 2.
All inputs are finite; a program needn't handle non-finite values.
Results may differ from a plain program's by a relative error of at most 0.0039.
Values may be sent and summed in bfloat16 or wider, within the bound.
No kernel may reach another device: no remote copies, remote signals or barrier semaphores. Data moves between devices by JAX's collectives and lax.ppermute only.
A program may use at most 64 MiB of HBM per device.

v0:
```python
import jax
import jax.numpy as jnp
from jax import lax
from jax.experimental import pallas as pl
from jax.experimental.pallas import tpu as pltpu
from jax.sharding import Mesh, PartitionSpec as P

BLOCK = 128
HALO = 128
SPAN = 256
EDGE = 256
CODE = 32
NONE = 4096
GROUP = 3


def shifted(x, axis, by):
    length = lax.axis_size(axis)
    pairs = [(i, i + by) for i in range(length) if 0 <= i + by < length]
    return lax.ppermute(x, axis, pairs)


SWAP = [(0, 1), (1, 0)]
PLANE = ("yh", "yl", "x")
BLOCKS = ("yl", "z", "x")
REGIONS = ("yh", "core")


def fine_mesh(mesh):
    return Mesh(mesh.devices.reshape(2, 2, 2, 8, 4), ("yh", "core", "yl", "z", "x"))


def reduce_everywhere(own, other):
    core = lax.axis_index("core")
    lanes = own.shape[1]
    own = own + lax.ppermute(other, "core", SWAP).astype(jnp.float32)
    count = lax.axis_size(PLANE)
    parts = own.astype(jnp.bfloat16).reshape(count, -1, lanes)
    parts = lax.all_to_all(parts, PLANE, 0, 0, tiled=True)
    own = parts.astype(jnp.float32).sum(0)
    size = lax.axis_size("z")
    for flip in (1, 2, 7):
        own = own + lax.ppermute(own, "z", [(i, i ^ flip) for i in range(size)])
    parts = jnp.broadcast_to(own.astype(jnp.bfloat16)[None], (count,) + own.shape)
    parts = lax.all_to_all(parts, PLANE, 0, 0, tiled=True).reshape(-1, lanes)
    other = lax.ppermute(parts, "core", SWAP)
    first = jnp.where(core == 0, parts, other)
    second = jnp.where(core == 0, other, parts)
    return first.astype(jnp.float32), second.astype(jnp.float32)


def dsilu(hidden):
    sigma = jax.nn.sigmoid(hidden)
    return sigma * (1.0 + hidden * (1.0 - sigma))


def fill_ids(ids_ref):
    ids_ref[...] = lax.broadcasted_iota(jnp.int32, ids_ref.shape, 0).astype(jnp.float32).astype(jnp.bfloat16)


def one_hot(ids_ref, entries):
    place = (entries & (SPAN - 1)).astype(jnp.float32).astype(jnp.bfloat16)
    return jnp.where(ids_ref[...] == place, jnp.ones((), jnp.bfloat16), jnp.zeros((), jnp.bfloat16))


def over_offsets(offsets, chans, step):
    def group(index, carry):
        for inner in range(GROUP):
            k = index * GROUP + inner
            step(k, pl.ds(pl.multiple_of(k * chans, chans), chans))
        return carry

    lax.fori_loop(0, offsets // GROUP, group, 0)


def gather_into(picked_ref, rule_ref, ids_ref, tiles, offsets, start, shift):
    chans = tiles[0].shape[0]
    sides = [jnp.concatenate([a, b], 0) for a, b in zip(tiles[:-1], tiles[1:])]

    def step(k, at):
        for q, side in enumerate(sides):
            entries = rule_ref[pl.ds(k, 1), start + SPAN * q : start + SPAN * (q + 1)] - shift
            both = jnp.dot(side, one_hot(ids_ref, entries), preferred_element_type=jnp.float32)
            half = lax.shift_right_arithmetic(entries, 8)
            found = jnp.where(half == q, both[:chans], jnp.where(half == q + 1, both[chans:], 0.0))
            picked_ref[at, SPAN * q : SPAN * (q + 1)] = found.astype(jnp.bfloat16)

    over_offsets(offsets, chans, step)


def side_by_side(w_ref, out_ref, turned):
    offsets, chans, _ = w_ref.shape
    for k in range(offsets):
        out_ref[:, k * chans : (k + 1) * chans] = w_ref[k].T if turned else w_ref[k]


def scatter_to(high_ref, low_ref, rule_ref, ids_ref, sources, w_ref, offsets, start, shift):
    chans = sources[0].shape[0]
    last = len(sources) - 1

    def put(at, q, tile):
        first = tile.astype(jnp.bfloat16)
        high_ref[at, SPAN * q : SPAN * (q + 1)] = first
        low_ref[at, SPAN * q : SPAN * (q + 1)] = (tile - first.astype(jnp.float32)).astype(jnp.bfloat16)

    def step(k, at):
        above = None
        for q, source in enumerate(sources):
            entries = rule_ref[pl.ds(k, 1), start + SPAN * q : start + SPAN * (q + 1)] + shift
            half = lax.shift_right_arithmetic(entries, 8)
            none = jnp.zeros((), jnp.bfloat16)
            parts = [] if q == 0 else [jnp.where(half == q, source, none)]
            if q < last:
                parts.append(jnp.where(half == q + 1, source, none))
            spread = lax.dot_general(
                jnp.concatenate(parts, 0) if len(parts) > 1 else parts[0],
                one_hot(ids_ref, entries),
                (((1,), (1,)), ((), ())),
                preferred_element_type=jnp.float32,
            )
            if q > 0:
                put(at, q - 1, above + spread[:chans])
            above = spread[-chans:]

    over_offsets(offsets, chans, step)
    used = SPAN * last
    total = jnp.dot(w_ref[...], high_ref[:, :used], preferred_element_type=jnp.float32)
    return total + jnp.dot(w_ref[...], low_ref[:, :used], preferred_element_type=jnp.float32)


def pack_kernel(feat_ref, grad_ref, rule_ref, own_ref, first_ref, last_ref):
    rows, chans = feat_ref.shape
    offsets = rule_ref.shape[0]
    own_ref[2 * chans :, :] = jnp.zeros((2 * CODE, rows), jnp.bfloat16)
    for b in range(rows // BLOCK):
        at = slice(b * BLOCK, (b + 1) * BLOCK)
        own_ref[:chans, at] = feat_ref[at, :].T
        own_ref[chans : 2 * chans, at] = grad_ref[at, :].T
    entries = rule_ref[...]
    code = jnp.where(entries == rows + 2 * HALO, 0, entries + 1)
    coarse = lax.shift_right_logical(code, 5).astype(jnp.float32).astype(jnp.bfloat16)
    fine = (code & 31).astype(jnp.float32).astype(jnp.bfloat16)
    own_ref[2 * chans : 2 * chans + offsets, :] = coarse
    own_ref[2 * chans + CODE : 2 * chans + CODE + offsets, :] = fine
    first_ref[...] = own_ref[:, :EDGE]
    last_ref[...] = own_ref[:, rows - EDGE :]


def grads_kernel(
    own_ref, before_ref, after_ref, grad_out_ref, w1_ref, w2_ref, core_ref,
    mine_ref, other_ref, source_ref, rule_ref,
    high_ref, low_ref, picked_ref, w_ref, ids_ref,
):
    rows, chans = grad_out_ref.shape
    offsets = mine_ref.shape[0] // chans
    wide = rows + 2 * HALO
    fill_ids(ids_ref)
    pieces = ((before_ref, -HALO - rows + EDGE), (own_ref, EDGE - HALO), (after_ref, EDGE - HALO + rows))
    column = 0
    for piece, base in pieces:
        coarse = piece[2 * chans : 2 * chans + CODE, :].astype(jnp.float32)
        fine = piece[2 * chans + CODE :, :].astype(jnp.float32)
        code = (coarse * 32.0 + fine).astype(jnp.int32)
        rule_ref[:, column : column + code.shape[1]] = jnp.where(code == 0, NONE, code - 1 + base)
        column += code.shape[1]

    def tiles(top):
        rest = slice(top, top + chans)
        inner = [own_ref[rest, SPAN * p : SPAN * (p + 1)] for p in range(rows // SPAN)]
        return [before_ref[rest, :]] + inner + [after_ref[rest, :]]

    side_by_side(w2_ref, w_ref, False)
    grad_act = scatter_to(
        high_ref, low_ref, rule_ref, ids_ref, tiles(chans), w_ref, offsets, 0, HALO
    )
    side_by_side(w1_ref, w_ref, True)
    gather_into(picked_ref, rule_ref, ids_ref, tiles(0), offsets, HALO, 0)
    hidden = jnp.dot(w_ref[...], picked_ref[...], preferred_element_type=jnp.float32)
    act = (hidden * jax.nn.sigmoid(hidden)).astype(jnp.bfloat16)
    grad_hidden = (grad_act * dsilu(hidden)).astype(jnp.bfloat16)
    source_ref[...] = grad_hidden
    inside = slice(HALO, HALO + rows)
    first = lax.dot_general(
        picked_ref[:, inside], grad_hidden[:, inside], (((1,), (1,)), ((), ())), preferred_element_type=jnp.float32
    )

    @pl.when(core_ref[0] == 0)
    def _():
        mine_ref[...] = first

    @pl.when(core_ref[0] != 0)
    def _():
        other_ref[...] = first.astype(jnp.bfloat16)

    act_tiles = [act[:, SPAN * q : SPAN * (q + 1)] for q in range(wide // SPAN)]
    gather_into(high_ref, rule_ref, ids_ref, act_tiles, offsets, EDGE, EDGE - HALO)
    second = jnp.dot(high_ref[:, :rows], grad_out_ref[...], preferred_element_type=jnp.float32)

    @pl.when(core_ref[0] != 0)
    def _():
        mine_ref[...] = second

    @pl.when(core_ref[0] == 0)
    def _():
        other_ref[...] = second.astype(jnp.bfloat16)


def input_grad_kernel(
    source_ref, rule_ref, w1_ref, grad_out_ref, live_ref, out_ref, high_ref, low_ref, w_ref, ids_ref
):
    rows, _ = grad_out_ref.shape
    offsets = w1_ref.shape[0]
    fill_ids(ids_ref)
    side_by_side(w1_ref, w_ref, False)
    sources = [source_ref[:, SPAN * q : SPAN * (q + 1)] for q in range(source_ref.shape[1] // SPAN)]
    total = scatter_to(high_ref, low_ref, rule_ref, ids_ref, sources, w_ref, offsets, HALO, 0)
    for b in range(rows // BLOCK):
        at = slice(b * BLOCK, (b + 1) * BLOCK)
        added = grad_out_ref[at, :].astype(jnp.float32) + total[:, at].T
        out_ref[at, :] = (live_ref[b].astype(jnp.float32) * added).astype(jnp.bfloat16)


def call(kernel, outs, scratch, *args, scalars=0, flops=0):
    vmem = pl.BlockSpec(memory_space=pltpu.VMEM)
    smem = pl.BlockSpec(memory_space=pltpu.SMEM)
    shapes = [jax.ShapeDtypeStruct(shape, dtype) for shape, dtype in outs]
    moved = sum(x.size * x.dtype.itemsize for x in (*args, *shapes))
    return pl.pallas_call(
        kernel,
        out_shape=shapes,
        in_specs=[vmem] * (len(args) - scalars) + [smem] * scalars,
        out_specs=[vmem] * len(outs),
        scratch_shapes=[pltpu.VMEM(shape, dtype) for shape, dtype in scratch],
        cost_estimate=pl.CostEstimate(flops=flops, bytes_accessed=moved, transcendentals=0),
    )(*args)


def on_device(features, grad_out, w1, w2, rulebook, live_blocks):
    rows, chans = features.shape
    offsets = w1.shape[0]
    wide = rows + 2 * HALO
    flat = offsets * chans
    bf16, f32, i32 = (jnp.bfloat16, jnp.float32, jnp.int32)
    ids = ((SPAN, SPAN), bf16)
    spread = ((flat, wide), bf16)
    beside = ((chans, flat), bf16)
    tall = 2 * chans + 2 * CODE
    one_pass = 2 * offsets * rows * SPAN * SPAN
    own, first, last = call(
        pack_kernel,
        [((tall, rows), bf16), ((tall, EDGE), bf16), ((tall, EDGE), bf16)],
        [],
        features,
        grad_out,
        rulebook,
    )
    before = shifted(last, BLOCKS, 1)
    after = shifted(first, BLOCKS, -1)
    core = lax.axis_index("core").astype(i32).reshape(1)
    mine, other, grad_hidden, wide_rules = call(
        grads_kernel,
        [((flat, chans), f32), ((flat, chans), bf16), ((chans, wide), bf16), ((CODE, rows + 2 * EDGE), i32)],
        [spread, spread, spread, beside, ids],
        own,
        before,
        after,
        grad_out,
        w1,
        w2,
        core,
        scalars=1,
        flops=6 * one_pass,
    )
    (grad_in,) = call(
        input_grad_kernel,
        [((rows, chans), bf16)],
        [((flat, rows), bf16), ((flat, rows), bf16), beside, ids],
        grad_hidden,
        wide_rules,
        w1,
        grad_out,
        live_blocks,
        scalars=1,
        flops=2 * one_pass,
    )
    kern_one, kern_two = reduce_everywhere(mine, other)
    voxel_total = rows * lax.axis_size(REGIONS) * lax.axis_size(BLOCKS)
    scale = jnp.sqrt(jnp.float32(voxel_total))
    return (grad_in, kern_one.reshape(w1.shape) / scale, kern_two.reshape(w1.shape) / scale)


def solution(mesh):
    rows = P(REGIONS + BLOCKS)

    return jax.shard_map(
        on_device,
        mesh=fine_mesh(mesh),
        in_specs=(rows, rows, P(), P(), P(None, REGIONS + BLOCKS), rows),
        out_specs=(rows, P(), P()),
        check_vma=False,
    )
```

profile of v0, /device:TPU:1, one launch (start us, length us, event | category | flops | bytes accessed | tf_op | source)
XLA Modules:
  0.0 123.9 jit_solution(11858484248449450589)
XLA Ops:
  0.6 2.1 %shard_map.85 = (bf16[320,768]{1,0:T(8,128)(2,1)}, bf16[320,256]{1,0:T(8,128)(2,1)}, bf16[320,256]{1,0:T(8,128)(2,1)}) custom-call(bf16[768,128]{1,0:T(8,128)(2,1)} %feat_ref.1, bf16[768,128]{1,0:T(8,128)(2,1)} %grad_out_ref.3, s32[27,768]{1,0:T(8,128)} %rule_ref.1), custom_call_target="tpu_custom_call" | custom-call | bytes 1295360 | tf_op jit(solution)/shard_map/pallas_call | solution.py:228
  2.7 3.9 %collective-permute-start = (bf16[320,256]{1,0:T(8,128)(2,1)}, bf16[320,256]{1,0:T(8,128)(2,1)S(1)}, u32[]{:S(2)}, u32[]{:S(2)}) collective-permute-start(bf16[320,256]{1,0:T(8,128)(2,1)} %get-tuple-element.11), channel_id=1, source_target_pairs={{0,1},{1,2},{2,3},{3,4},{4,5},{5,6},{6,7},{7,8},{8,9},{9,10},{10,1... | collective-permute-start | bytes 491528 | tf_op jit(solution)/shard_map/ppermute | solution.py:20
  6.7 1.3 %collective-permute-start.1 = (bf16[320,256]{1,0:T(8,128)(2,1)}, bf16[320,256]{1,0:T(8,128)(2,1)S(1)}, u32[]{:S(2)}, u32[]{:S(2)}) collective-permute-start(bf16[320,256]{1,0:T(8,128)(2,1)} %get-tuple-element.12), channel_id=1, source_target_pairs={{1,0},{2,1},{3,2},{4,3},{5,4},{6,5},{7,6},{8,7},{9,8},{10,9},{11,1... | collective-permute-start | bytes 491528 | tf_op jit(solution)/shard_map/ppermute | solution.py:20
  8.0 1.9 %collective-permute-done.before_ref = bf16[320,256]{1,0:T(8,128)(2,1)S(1)} collective-permute-done((bf16[320,256]{1,0:T(8,128)(2,1)}, bf16[320,256]{1,0:T(8,128)(2,1)S(1)}, u32[]{:S(2)}, u32[]{:S(2)}) %collective-permute-start) | collective-permute-done | bytes 163872 | tf_op jit(solution)/shard_map/ppermute | solution.py:20
  9.8 0.0 copy-start
  9.8 3.7 %collective-permute-done.1.after_ref = bf16[320,256]{1,0:T(8,128)(2,1)S(1)} collective-permute-done((bf16[320,256]{1,0:T(8,128)(2,1)}, bf16[320,256]{1,0:T(8,128)(2,1)S(1)}, u32[]{:S(2)}, u32[]{:S(2)}) %collective-permute-start.1) | collective-permute-done | bytes 163872 | tf_op jit(solution)/shard_map/ppermute | solution.py:20
  13.6 0.0 copy-start.1
  13.6 0.0 copy-done
  13.6 0.7 copy-done.1
  14.2 27.2 %shard_map.86 = (f32[3456,128]{1,0:T(8,128)}, bf16[3456,128]{1,0:T(8,128)(2,1)}, bf16[128,1024]{1,0:T(8,128)(2,1)}, s32[32,1280]{1,0:T(8,128)}) custom-call(bf16[320,768]{1,0:T(8,128)(2,1)} %get-tuple-element.10.own_ref, bf16[320,256]{1,0:T(8,128)(2,1)} %copy-done, bf16[320,256]{1,0:T(8,128)(2,1)} %copy-done.1, bf16[768,128]{1,0:T(8,128)(2,1)} %grad_out_ref.3, ...), custom_call_target="tpu_custom_call" | custom-call | flops 16307453952 | bytes 5865476 | tf_op jit(solution)/shard_map/pallas_call | solution.py:228
  41.4 1.8 %collective-permute-start.2 = (bf16[3456,128]{1,0:T(8,128)(2,1)}, bf16[3456,128]{1,0:T(8,128)(2,1)S(1)}, u32[]{:S(2)}, u32[]{:S(2)}) collective-permute-start(bf16[3456,128]{1,0:T(8,128)(2,1)} %get-tuple-element.16), channel_id=1, source_target_pairs={{0,64},{64,0},{1,65},{65,1},{2,66},{66,2},{3,67},{67,3},{4,68},{68... | collective-permute-start | bytes 2654216 | tf_op jit(solution)/shard_map/ppermute | solution.py:36
  43.2 2.3 %collective-permute-done.2 = bf16[3456,128]{1,0:T(8,128)(2,1)S(1)} collective-permute-done((bf16[3456,128]{1,0:T(8,128)(2,1)}, bf16[3456,128]{1,0:T(8,128)(2,1)S(1)}, u32[]{:S(2)}, u32[]{:S(2)}) %collective-permute-start.2) | collective-permute-done | bytes 884768 | tf_op jit(solution)/shard_map/ppermute | solution.py:36
  45.5 1.7 %add_convert_fusion = bf16[3456,128]{1,0:T(8,128)(2,1)S(1)} fusion(f32[3456,128]{1,0:T(8,128)} %get-tuple-element.15, bf16[3456,128]{1,0:T(8,128)(2,1)S(1)} %collective-permute-done.2), kind=kLoop, calls=%fused_computation.3 | loop fusion | flops 1327104 | bytes 3538944 | tf_op jit(solution)/shard_map/convert_element_type | solution.py:38
  47.2 23.6 %all_to_all.10 = bf16[16,216,128]{2,1,0:T(8,128)(2,1)S(1)} all-to-all(bf16[16,216,128]{2,1,0:T(8,128)(2,1)S(1)} %bitcast.7), channel_id=1, replica_groups=mesh['yh'=2,'core'=2,'yl'=2,'z'=8,'x'=4] {'yh','yl','x'}, dimensions={0} | all-to-all | bytes 1769472 | tf_op jit(solution)/shard_map/all_to_all | solution.py:39
  70.8 0.1 convert_reduce_fusion
  70.9 1.7 %collective-permute-start.3 = (f32[216,128]{1,0:T(8,128)S(1)}, f32[216,128]{1,0:T(8,128)S(1)}, u32[]{:S(2)}, u32[]{:S(2)}) collective-permute-start(f32[216,128]{1,0:T(8,128)S(1)} %convert_reduce_fusion), channel_id=1, source_target_pairs={{0,4},{4,0},{8,12},{12,8},{16,20},{20,16},{24,28},{28,24},{1,5},{5... | collective-permute-start | bytes 331784 | tf_op jit(solution)/shard_map/ppermute | solution.py:43
  72.7 2.1 %collective-permute-done.3 = f32[216,128]{1,0:T(8,128)S(1)} collective-permute-done((f32[216,128]{1,0:T(8,128)S(1)}, f32[216,128]{1,0:T(8,128)S(1)}, u32[]{:S(2)}, u32[]{:S(2)}) %collective-permute-start.3) | collective-permute-done | bytes 110624 | tf_op jit(solution)/shard_map/ppermute | solution.py:43
  74.8 5.5 %collective-permute-start.4 = (f32[216,128]{1,0:T(8,128)S(1)}, f32[216,128]{1,0:T(8,128)S(1)}, u32[]{:S(2)}, u32[]{:S(2)}) collective-permute-start(f32[216,128]{1,0:T(8,128)S(1)} %add.13), channel_id=1, source_target_pairs={{0,8},{4,12},{8,0},{12,4},{16,24},{20,28},{24,16},{28,20},{1,9},{5... | collective-permute-start | bytes 331784 | tf_op jit(solution)/shard_map/ppermute | solution.py:43
  80.3 2.1 %collective-permute-done.4 = f32[216,128]{1,0:T(8,128)S(1)} collective-permute-done((f32[216,128]{1,0:T(8,128)S(1)}, f32[216,128]{1,0:T(8,128)S(1)}, u32[]{:S(2)}, u32[]{:S(2)}) %collective-permute-start.4) | collective-permute-done | bytes 110624 | tf_op jit(solution)/shard_map/ppermute | solution.py:43
  82.5 3.9 %collective-permute-start.5 = (f32[216,128]{1,0:T(8,128)S(1)}, f32[216,128]{1,0:T(8,128)S(1)}, u32[]{:S(2)}, u32[]{:S(2)}) collective-permute-start(f32[216,128]{1,0:T(8,128)S(1)} %add.14), channel_id=1, source_target_pairs={{0,28},{4,24},{8,20},{12,16},{16,12},{20,8},{24,4},{28,0},{1,29},{... | collective-permute-start | bytes 331784 | tf_op jit(solution)/shard_map/ppermute | solution.py:43
  86.4 2.7 %collective-permute-done.5 = f32[216,128]{1,0:T(8,128)S(1)} collective-permute-done((f32[216,128]{1,0:T(8,128)S(1)}, f32[216,128]{1,0:T(8,128)S(1)}, u32[]{:S(2)}, u32[]{:S(2)}) %collective-permute-start.5) | collective-permute-done | bytes 110624 | tf_op jit(solution)/shard_map/ppermute | solution.py:43
  89.1 0.1 broadcast_in_dim.2
  89.2 18.7 %all_to_all.11 = bf16[16,216,128]{2,1,0:T(8,128)(2,1)S(1)} all-to-all(bf16[16,216,128]{2,1,0:T(8,128)(2,1)S(1)} %broadcast_in_dim.2), channel_id=1, replica_groups=mesh['yh'=2,'core'=2,'yl'=2,'z'=8,'x'=4] {'yh','yl','x'}, dimensions={0} | all-to-all | bytes 1769472 | tf_op jit(solution)/shard_map/all_to_all | solution.py:45
  107.9 3.8 %collective-permute-start.6 = (bf16[3456,128]{1,0:T(8,128)(2,1)S(1)}, bf16[3456,128]{1,0:T(8,128)(2,1)S(1)}, u32[]{:S(2)}, u32[]{:S(2)}) collective-permute-start(bf16[3456,128]{1,0:T(8,128)(2,1)S(1)} %bitcast.8), channel_id=1, source_target_pairs={{0,64},{64,0},{1,65},{65,1},{2,66},{66,2},{3,67},{67,3},{4,68},{68... | collective-permute-start | bytes 2654216 | tf_op jit(solution)/shard_map/ppermute | solution.py:46
  111.7 10.0 %shard_map.87 = bf16[768,128]{1,0:T(8,128)(2,1)} custom-call(bf16[128,1024]{1,0:T(8,128)(2,1)} %get-tuple-element.13.source_ref, s32[32,1280]{1,0:T(8,128)} %get-tuple-element.14.rule_ref, bf16[27,128,128]{2,1,0:T(8,128)(2,1)} %w1_ref.3, bf16[768,128]{1,0:T(8,128)(2,1)} %grad_out_ref.3, s32[6]{0:T(128)} %live_ref.1), custom_call_target="tpu_custom_call" | custom-call | flops 5435817984 | bytes 1703960 | tf_op jit(solution)/shard_map/pallas_call | solution.py:228
  121.7 0.0 collective-permute-done.6
  121.7 2.2 %convert_multiply_fusion = (f32[3456,128]{1,0:T(8,128)}, f32[3456,128]{1,0:T(8,128)}) fusion(bf16[3456,128]{1,0:T(8,128)(2,1)S(1)} %collective-permute-done.6, pred[]{:T(512)S(6)} %eq.4, bf16[16,216,128]{2,1,0:T(8,128)(2,1)S(1)} %all_to_all.11), kind=kLoop, calls=%fused_computation | loop fusion | flops 2654208 | bytes 5308417 | tf_op jit(solution)/shard_map/div | solution.py:289
  (3 shorter events, 0.0 us)
Async XLA Ops:
  2.7 7.1 %collective-permute-start = (bf16[320,256]{1,0:T(8,128)(2,1)}, bf16[320,256]{1,0:T(8,128)(2,1)S(1)}, u32[]{:S(2)}, u32[]{:S(2)}) collective-permute-start(bf16[320,256]{1,0:T(8,128)(2,1)} %get-tuple-element.11), channel_id=1, source_target_pairs={{0,1},{1,2},{2,3},{3,4},{4,5},{5,6},{6,7},{7,8},{8,9},{9,10},{10,1... | collective-permute-start | bytes 491528 | tf_op jit(solution)/shard_map/ppermute | solution.py:20
  6.7 6.9 %collective-permute-start.1 = (bf16[320,256]{1,0:T(8,128)(2,1)}, bf16[320,256]{1,0:T(8,128)(2,1)S(1)}, u32[]{:S(2)}, u32[]{:S(2)}) collective-permute-start(bf16[320,256]{1,0:T(8,128)(2,1)} %get-tuple-element.12), channel_id=1, source_target_pairs={{1,0},{2,1},{3,2},{4,3},{5,4},{6,5},{7,6},{8,7},{9,8},{10,9},{11,1... | collective-permute-start | bytes 491528 | tf_op jit(solution)/shard_map/ppermute | solution.py:20
  9.8 3.7 %copy-start = (bf16[320,256]{1,0:T(8,128)(2,1)}, bf16[320,256]{1,0:T(8,128)(2,1)S(1)}, u32[]{:S(2)}) copy-start(bf16[320,256]{1,0:T(8,128)(2,1)S(1)} %collective-permute-done.before_ref) | copy-start | bytes 491524
  13.6 0.7 copy-start.1
  41.4 4.1 %collective-permute-start.2 = (bf16[3456,128]{1,0:T(8,128)(2,1)}, bf16[3456,128]{1,0:T(8,128)(2,1)S(1)}, u32[]{:S(2)}, u32[]{:S(2)}) collective-permute-start(bf16[3456,128]{1,0:T(8,128)(2,1)} %get-tuple-element.16), channel_id=1, source_target_pairs={{0,64},{64,0},{1,65},{65,1},{2,66},{66,2},{3,67},{67,3},{4,68},{68... | collective-permute-start | bytes 2654216 | tf_op jit(solution)/shard_map/ppermute | solution.py:36
  70.9 3.9 %collective-permute-start.3 = (f32[216,128]{1,0:T(8,128)S(1)}, f32[216,128]{1,0:T(8,128)S(1)}, u32[]{:S(2)}, u32[]{:S(2)}) collective-permute-start(f32[216,128]{1,0:T(8,128)S(1)} %convert_reduce_fusion), channel_id=1, source_target_pairs={{0,4},{4,0},{8,12},{12,8},{16,20},{20,16},{24,28},{28,24},{1,5},{5... | collective-permute-start | bytes 331784 | tf_op jit(solution)/shard_map/ppermute | solution.py:43
  74.8 7.6 %collective-permute-start.4 = (f32[216,128]{1,0:T(8,128)S(1)}, f32[216,128]{1,0:T(8,128)S(1)}, u32[]{:S(2)}, u32[]{:S(2)}) collective-permute-start(f32[216,128]{1,0:T(8,128)S(1)} %add.13), channel_id=1, source_target_pairs={{0,8},{4,12},{8,0},{12,4},{16,24},{20,28},{24,16},{28,20},{1,9},{5... | collective-permute-start | bytes 331784 | tf_op jit(solution)/shard_map/ppermute | solution.py:43
  82.5 6.6 %collective-permute-start.5 = (f32[216,128]{1,0:T(8,128)S(1)}, f32[216,128]{1,0:T(8,128)S(1)}, u32[]{:S(2)}, u32[]{:S(2)}) collective-permute-start(f32[216,128]{1,0:T(8,128)S(1)} %add.14), channel_id=1, source_target_pairs={{0,28},{4,24},{8,20},{12,16},{16,12},{20,8},{24,4},{28,0},{1,29},{... | collective-permute-start | bytes 331784 | tf_op jit(solution)/shard_map/ppermute | solution.py:43
  107.9 13.8 %collective-permute-start.6 = (bf16[3456,128]{1,0:T(8,128)(2,1)S(1)}, bf16[3456,128]{1,0:T(8,128)(2,1)S(1)}, u32[]{:S(2)}, u32[]{:S(2)}) collective-permute-start(bf16[3456,128]{1,0:T(8,128)(2,1)S(1)} %bitcast.8), channel_id=1, source_target_pairs={{0,64},{64,0},{1,65},{65,1},{2,66},{66,2},{3,67},{67,3},{4,68},{68... | collective-permute-start | bytes 2654216 | tf_op jit(solution)/shard_map/ppermute | solution.py:46
where the time goes:
time: 124 us
  blocking collectives  42.4 us (34%)
  Pallas kernels  39.3 us (32%)
  starting transfers between devices  21.9 us (18%)
  waiting for transfers between devices  14.8 us (12%)
  other arithmetic  4.06 us (3%)
    pallas_call x3, Pallas kernels, call(): pl.pallas_call(kernel, out_shape=shapes, in_specs=[vmem] * (len(args) - s...  39.3 us
    all_to_all x1, blocking collectives, reduce_everywhere(): parts = lax.all_to_all(parts, PLANE, 0, 0, tiled=True)  23.6 us
    all_to_all x1, blocking collectives, reduce_everywhere(): parts = lax.all_to_all(parts, PLANE, 0, 0, tiled=True).reshape(-1, lanes)  18.7 us
    ppermute x3, starting transfers between devices, reduce_everywhere(): own = own + lax.ppermute(own, 'z', [(i, i ^ flip) for i in range(size)])  11.1 us
    ppermute x3, waiting for transfers between devices, reduce_everywhere(): own = own + lax.ppermute(own, 'z', [(i, i ^ flip) for i in range(size)])  6.98 us
    ppermute x2, waiting for transfers between devices, shifted(): return lax.ppermute(x, axis, pairs)  5.6 us
    ppermute x2, starting transfers between devices, shifted(): return lax.ppermute(x, axis, pairs)  5.22 us
    ppermute x1, starting transfers between devices, reduce_everywhere(): other = lax.ppermute(parts, 'core', SWAP)  3.77 us
  transfers between devices with their start and end apart: 7, of which 6 were waited for; matrix products, arithmetic and copies ran while one was open for 0% of the time, Pallas kernels for 8%

commit v1 on v0

--- a/solution.py
+++ b/solution.py
@@ -11,23 +11,23 @@
 EDGE = 256
 CODE = 32
 NONE = 4096
-GROUP = 3
-
-
-def shifted(x, axis, by):
+GROUP = 9
+
+
+def swapped(x, axis, odd):
     length = lax.axis_size(axis)
-    pairs = [(i, i + by) for i in range(length) if 0 <= i + by < length]
-    return lax.ppermute(x, axis, pairs)
+    pairs = [(i, ((i + odd) ^ 1) - odd) for i in range(length)]
+    return lax.ppermute(x, axis, [(i, j) for i, j in pairs if 0 <= j < length])
 
 
 SWAP = [(0, 1), (1, 0)]
-PLANE = ("yh", "yl", "x")
-BLOCKS = ("yl", "z", "x")
+PLANE = ("yh", "yl", "z_lo", "x")
+BLOCKS = ("yl", "z_hi", "z_lo", "x")
 REGIONS = ("yh", "core")
 
 
 def fine_mesh(mesh):
-    return Mesh(mesh.devices.reshape(2, 2, 2, 8, 4), ("yh", "core", "yl", "z", "x"))
+    return Mesh(mesh.devices.reshape(2, 2, 2, 4, 2, 4), ("yh", "core", "yl", "z_hi", "z_lo", "x"))
 
 
 def reduce_everywhere(own, other):
@@ -38,9 +38,8 @@
     parts = own.astype(jnp.bfloat16).reshape(count, -1, lanes)
     parts = lax.all_to_all(parts, PLANE, 0, 0, tiled=True)
     own = parts.astype(jnp.float32).sum(0)
-    size = lax.axis_size("z")
-    for flip in (1, 2, 7):
-        own = own + lax.ppermute(own, "z", [(i, i ^ flip) for i in range(size)])
+    for flip in (1, 3):
+        own = own + lax.ppermute(own, "z_hi", [(i, i ^ flip) for i in range(lax.axis_size("z_hi"))])
     parts = jnp.broadcast_to(own.astype(jnp.bfloat16)[None], (count,) + own.shape)
     parts = lax.all_to_all(parts, PLANE, 0, 0, tiled=True).reshape(-1, lanes)
     other = lax.ppermute(parts, "core", SWAP)
@@ -128,7 +127,7 @@
     return total + jnp.dot(w_ref[...], low_ref[:, :used], preferred_element_type=jnp.float32)
 
 
-def pack_kernel(feat_ref, grad_ref, rule_ref, own_ref, first_ref, last_ref):
+def pack_kernel(feat_ref, grad_ref, rule_ref, odd_ref, own_ref, to_even_ref, to_odd_ref):
     rows, chans = feat_ref.shape
     offsets = rule_ref.shape[0]
     own_ref[2 * chans :, :] = jnp.zeros((2 * CODE, rows), jnp.bfloat16)
@@ -142,19 +141,24 @@
     fine = (code & 31).astype(jnp.float32).astype(jnp.bfloat16)
     own_ref[2 * chans : 2 * chans + offsets, :] = coarse
     own_ref[2 * chans + CODE : 2 * chans + CODE + offsets, :] = fine
-    first_ref[...] = own_ref[:, :EDGE]
-    last_ref[...] = own_ref[:, rows - EDGE :]
+    first, last = own_ref[:, :EDGE], own_ref[:, rows - EDGE :]
+    odd = odd_ref[0] == 1
+    to_even_ref[...] = jnp.where(odd, first, last)
+    to_odd_ref[...] = jnp.where(odd, last, first)
 
 
 def grads_kernel(
-    own_ref, before_ref, after_ref, grad_out_ref, w1_ref, w2_ref, core_ref,
+    own_ref, even_ref, odd_ref, grad_out_ref, w1_ref, w2_ref, core_ref, parity_ref,
     mine_ref, other_ref, source_ref, rule_ref,
-    high_ref, low_ref, picked_ref, w_ref, ids_ref,
+    high_ref, low_ref, picked_ref, w_ref, before_ref, after_ref, ids_ref,
 ):
     rows, chans = grad_out_ref.shape
     offsets = mine_ref.shape[0] // chans
     wide = rows + 2 * HALO
     fill_ids(ids_ref)
+    is_odd = parity_ref[0] == 1
+    before_ref[...] = jnp.where(is_odd, even_ref[...], odd_ref[...])
+    after_ref[...] = jnp.where(is_odd, odd_ref[...], even_ref[...])
     pieces = ((before_ref, -HALO - rows + EDGE), (own_ref, EDGE - HALO), (after_ref, EDGE - HALO + rows))
     column = 0
     for piece, base in pieces:
@@ -246,29 +250,33 @@
     beside = ((chans, flat), bf16)
     tall = 2 * chans + 2 * CODE
     one_pass = 2 * offsets * rows * SPAN * SPAN
-    own, first, last = call(
+    parity = (lax.axis_index("x").astype(i32) & 1).reshape(1)
+    own, to_even, to_odd = call(
         pack_kernel,
         [((tall, rows), bf16), ((tall, EDGE), bf16), ((tall, EDGE), bf16)],
         [],
         features,
         grad_out,
         rulebook,
-    )
-    before = shifted(last, BLOCKS, 1)
-    after = shifted(first, BLOCKS, -1)
+        parity,
+        scalars=1,
+    )
+    even = swapped(to_even, BLOCKS, 0)
+    odd = swapped(to_odd, BLOCKS, 1)
     core = lax.axis_index("core").astype(i32).reshape(1)
     mine, other, grad_hidden, wide_rules = call(
         grads_kernel,
         [((flat, chans), f32), ((flat, chans), bf16), ((chans, wide), bf16), ((CODE, rows + 2 * EDGE), i32)],
-        [spread, spread, spread, beside, ids],
+        [spread, spread, spread, beside, ((tall, EDGE), bf16), ((tall, EDGE), bf16), ids],
         own,
-        before,
-        after,
+        even,
+        odd,
         grad_out,
         w1,
         w2,
         core,
-        scalars=1,
+        parity,
+        scalars=2,
         flops=6 * one_pass,
     )
     (grad_in,) = call(

time: 124 us -> 114 us (0.919)
  waiting for transfers between devices: 14.8 us -> 8.23 us
  Pallas kernels: 39.3 us -> 35.9 us
  starting transfers between devices: 21.9 us -> 20 us
    ppermute x5 -> x4, waiting for transfers between devices: 12.6 us -> 5.96 us  [the longest x2 3.65 us: reduce_everywhere(): lax.ppermute(own, 'z_hi', [(i, i ^ flip) for i in range(lax.axis_size('z_...]
    ppermute x5 -> x4, starting transfers between devices: 16.4 us -> 11.3 us  [the longest x2 8.61 us: reduce_everywhere(): lax.ppermute(own, 'z_hi', [(i, i ^ flip) for i in range(lax.axis_size('z_...]
    pallas_call x3, Pallas kernels: 39.3 us -> 35.9 us  [call(): pl.pallas_call(kernel, out_shape=shapes, in_specs=[vmem] * (len(args) - s...]
    all_to_all x1, blocking collectives: 23.6 us -> 26.4 us  [reduce_everywhere(): parts = lax.all_to_all(parts, PLANE, 0, 0, tiled=True)]
    ppermute x1, starting transfers between devices: 1.82 us -> 3.72 us  [reduce_everywhere(): own = own + lax.ppermute(other, 'core', SWAP).astype(jnp.float32)]
    all_to_all x1, blocking collectives: 18.7 us -> 17 us  [reduce_everywhere(): parts = lax.all_to_all(parts, PLANE, 0, 0, tiled=True).reshape(-1, lanes)]
  transfers between devices with their start and end apart: 7 -> 6, of which waited for: 6 -> 4; matrix products, arithmetic and copies ran while one was open for 0% -> 0% of each run, Pallas kernels for 8% -> 8%
where the time goes in v1:
time: 114 us; the launch traced here: 113 us
  blocking collectives  43.3 us (38%)
  Pallas kernels  35.9 us (31%)
  starting transfers between devices  20 us (18%)
  waiting for transfers between devices  8.23 us (7%)
  other arithmetic  3.99 us (4%)
    pallas_call x3, Pallas kernels, call(): pl.pallas_call(kernel, out_shape=shapes, in_specs=[vmem] * (len(args) - s...  35.9 us
    all_to_all x1, blocking collectives, reduce_everywhere(): parts = lax.all_to_all(parts, PLANE, 0, 0, tiled=True)  26.4 us
    all_to_all x1, blocking collectives, reduce_everywhere(): parts = lax.all_to_all(parts, PLANE, 0, 0, tiled=True).reshape(-1, lanes)  17 us
    ppermute x2, starting transfers between devices, reduce_everywhere(): lax.ppermute(own, 'z_hi', [(i, i ^ flip) for i in range(lax.axis_size('z_...  8.61 us
    ppermute x1, starting transfers between devices, reduce_everywhere(): other = lax.ppermute(parts, 'core', SWAP)  5.01 us
    ppermute x1, starting transfers between devices, reduce_everywhere(): own = own + lax.ppermute(other, 'core', SWAP).astype(jnp.float32)  3.72 us
    ppermute x2, waiting for transfers between devices, reduce_everywhere(): lax.ppermute(own, 'z_hi', [(i, i ^ flip) for i in range(lax.axis_size('z_...  3.65 us
    ppermute x2, starting transfers between devices, swapped(): return lax.ppermute(x, axis, [(i, j) for i, j in pairs if 0 <= j < length])  2.69 us
  transfers between devices with their start and end apart: 6, of which 4 were waited for; matrix products, arithmetic and copies ran while one was open for 0% of the time, Pallas kernels for 8%

profile of v1, /device:TPU:1, one launch (start us, length us, event | category | flops | bytes accessed | tf_op | source)
XLA Modules:
  0.0 113.3 jit_solution(4675742963192410510)
XLA Ops:
  0.6 2.1 %shard_map.85 = (bf16[320,768]{1,0:T(8,128)(2,1)}, bf16[320,256]{1,0:T(8,128)(2,1)}, bf16[320,256]{1,0:T(8,128)(2,1)}) custom-call(bf16[768,128]{1,0:T(8,128)(2,1)} %feat_ref.1, bf16[768,128]{1,0:T(8,128)(2,1)} %grad_out_ref.3, s32[27,768]{1,0:T(8,128)} %rule_ref.1, s32[1]{0:T(128)} %bitcast.odd_ref.parity_ref), custom_call_target="tpu_custom_call" | custom-call | bytes 1295364 | tf_op jit(solution)/shard_map/pallas_call | solution.py:232
  2.8 2.0 %collective-permute-start = (bf16[320,256]{1,0:T(8,128)(2,1)}, bf16[320,256]{1,0:T(8,128)(2,1)S(1)}, u32[]{:S(2)}, u32[]{:S(2)}) collective-permute-start(bf16[320,256]{1,0:T(8,128)(2,1)} %get-tuple-element.11), channel_id=1, source_target_pairs={{0,1},{1,0},{2,3},{3,2},{4,5},{5,4},{6,7},{7,6},{8,9},{9,8},{10,11... | collective-permute-start | bytes 491528 | tf_op jit(solution)/shard_map/ppermute | solution.py:20
  4.8 0.7 collective-permute-start.1
  5.5 2.3 %collective-permute-done.even_ref = bf16[320,256]{1,0:T(8,128)(2,1)S(1)} collective-permute-done((bf16[320,256]{1,0:T(8,128)(2,1)}, bf16[320,256]{1,0:T(8,128)(2,1)S(1)}, u32[]{:S(2)}, u32[]{:S(2)}) %collective-permute-start) | collective-permute-done | bytes 163872 | tf_op jit(solution)/shard_map/ppermute | solution.py:20
  7.8 0.0 copy-start
  7.8 0.0 collective-permute-done.1.odd_ref
  7.8 0.0 copy-start.1
  7.8 0.7 copy-done
  8.5 0.0 copy-done.1
  8.5 24.5 %shard_map.86 = (f32[3456,128]{1,0:T(8,128)}, bf16[3456,128]{1,0:T(8,128)(2,1)}, bf16[128,1024]{1,0:T(8,128)(2,1)}, s32[32,1280]{1,0:T(8,128)}) custom-call(bf16[320,768]{1,0:T(8,128)(2,1)} %get-tuple-element.10.own_ref, bf16[320,256]{1,0:T(8,128)(2,1)} %copy-done, bf16[320,256]{1,0:T(8,128)(2,1)} %copy-done.1, bf16[768,128]{1,0:T(8,128)(2,1)} %grad_out_ref.3, ...), custom_call_target="tpu_custom_call" | custom-call | flops 16307453952 | bytes 5865480 | tf_op jit(solution)/shard_map/pallas_call | solution.py:232
  33.0 3.7 %collective-permute-start.2 = (bf16[3456,128]{1,0:T(8,128)(2,1)}, bf16[3456,128]{1,0:T(8,128)(2,1)S(1)}, u32[]{:S(2)}, u32[]{:S(2)}) collective-permute-start(bf16[3456,128]{1,0:T(8,128)(2,1)} %get-tuple-element.16), channel_id=1, source_target_pairs={{0,64},{64,0},{1,65},{65,1},{2,66},{66,2},{3,67},{67,3},{4,68},{68... | collective-permute-start | bytes 2654216 | tf_op jit(solution)/shard_map/ppermute | solution.py:36
  36.8 2.3 %collective-permute-done.2 = bf16[3456,128]{1,0:T(8,128)(2,1)S(1)} collective-permute-done((bf16[3456,128]{1,0:T(8,128)(2,1)}, bf16[3456,128]{1,0:T(8,128)(2,1)S(1)}, u32[]{:S(2)}, u32[]{:S(2)}) %collective-permute-start.2) | collective-permute-done | bytes 884768 | tf_op jit(solution)/shard_map/ppermute | solution.py:36
  39.0 1.7 %add_convert_fusion = bf16[3456,128]{1,0:T(8,128)(2,1)S(1)} fusion(f32[3456,128]{1,0:T(8,128)} %get-tuple-element.15, bf16[3456,128]{1,0:T(8,128)(2,1)S(1)} %collective-permute-done.2), kind=kLoop, calls=%fused_computation.3 | loop fusion | flops 1327104 | bytes 3538944 | tf_op jit(solution)/shard_map/convert_element_type | solution.py:38
  40.7 0.2 reshape.27
  40.9 26.4 %all_to_all.10 = bf16[32,108,128]{2,1,0:T(8,128)(2,1)S(1)} all-to-all(bf16[32,108,128]{2,1,0:T(8,128)(2,1)S(1)} %reshape.27), channel_id=1, replica_groups=mesh['yh'=2,'core'=2,'yl'=2,'z_hi'=4,'z_lo'=2,'x'=4] {'yh','yl','z_lo','x'}, dimensions={0} | all-to-all | bytes 1769472 | tf_op jit(solution)/shard_map/all_to_all | solution.py:39
  67.3 0.1 convert_reduce_fusion
  67.4 3.6 %collective-permute-start.3 = (f32[108,128]{1,0:T(8,128)S(1)}, f32[108,128]{1,0:T(8,128)S(1)}, u32[]{:S(2)}, u32[]{:S(2)}) collective-permute-start(f32[108,128]{1,0:T(8,128)S(1)} %convert_reduce_fusion), channel_id=1, source_target_pairs={{0,8},{8,0},{16,24},{24,16},{1,9},{9,1},{17,25},{25,17},{2,10},{10... | collective-permute-start | bytes 165896 | tf_op jit(solution)/shard_map/ppermute | solution.py:42
  71.0 2.0 %collective-permute-done.3 = f32[108,128]{1,0:T(8,128)S(1)} collective-permute-done((f32[108,128]{1,0:T(8,128)S(1)}, f32[108,128]{1,0:T(8,128)S(1)}, u32[]{:S(2)}, u32[]{:S(2)}) %collective-permute-start.3) | collective-permute-done | bytes 55328 | tf_op jit(solution)/shard_map/ppermute | solution.py:42
  73.1 5.0 %collective-permute-start.4 = (f32[108,128]{1,0:T(8,128)S(1)}, f32[108,128]{1,0:T(8,128)S(1)}, u32[]{:S(2)}, u32[]{:S(2)}) collective-permute-start(f32[108,128]{1,0:T(8,128)S(1)} %add.10), channel_id=1, source_target_pairs={{0,24},{8,16},{16,8},{24,0},{1,25},{9,17},{17,9},{25,1},{2,26},{10... | collective-permute-start | bytes 165896 | tf_op jit(solution)/shard_map/ppermute | solution.py:42
  78.1 1.6 %collective-permute-done.4 = f32[108,128]{1,0:T(8,128)S(1)} collective-permute-done((f32[108,128]{1,0:T(8,128)S(1)}, f32[108,128]{1,0:T(8,128)S(1)}, u32[]{:S(2)}, u32[]{:S(2)}) %collective-permute-start.4) | collective-permute-done | bytes 55328 | tf_op jit(solution)/shard_map/ppermute | solution.py:42
  79.7 0.1 broadcast_in_dim.2
  79.8 17.0 %all_to_all.11 = bf16[32,108,128]{2,1,0:T(8,128)(2,1)S(1)} all-to-all(bf16[32,108,128]{2,1,0:T(8,128)(2,1)S(1)} %broadcast_in_dim.2), channel_id=1, replica_groups=mesh['yh'=2,'core'=2,'yl'=2,'z_hi'=4,'z_lo'=2,'x'=4] {'yh','yl','z_lo','x'}, dimensions={0} | all-to-all | bytes 1769472 | tf_op jit(solution)/shard_map/all_to_all | solution.py:44
  96.8 0.2 reshape.28
  96.9 5.0 %collective-permute-start.5 = (bf16[3456,128]{1,0:T(8,128)(2,1)S(1)}, bf16[3456,128]{1,0:T(8,128)(2,1)S(1)}, u32[]{:S(2)}, u32[]{:S(2)}) collective-permute-start(bf16[3456,128]{1,0:T(8,128)(2,1)S(1)} %reshape.28), channel_id=1, source_target_pairs={{0,64},{64,0},{1,65},{65,1},{2,66},{66,2},{3,67},{67,3},{4,68},{68... | collective-permute-start | bytes 2654216 | tf_op jit(solution)/shard_map/ppermute | solution.py:45
  101.9 9.2 %shard_map.87 = bf16[768,128]{1,0:T(8,128)(2,1)} custom-call(bf16[128,1024]{1,0:T(8,128)(2,1)} %get-tuple-element.13.source_ref, s32[32,1280]{1,0:T(8,128)} %get-tuple-element.14.rule_ref, bf16[27,128,128]{2,1,0:T(8,128)(2,1)} %w1_ref.3, bf16[768,128]{1,0:T(8,128)(2,1)} %grad_out_ref.3, s32[6]{0:T(128)} %live_ref.1), custom_call_target="tpu_custom_call" | custom-call | flops 5435817984 | bytes 1703960 | tf_op jit(solution)/shard_map/pallas_call | solution.py:232
  111.2 0.0 collective-permute-done.5
  111.2 2.1 %convert_multiply_fusion = (f32[3456,128]{1,0:T(8,128)}, f32[3456,128]{1,0:T(8,128)}) fusion(bf16[3456,128]{1,0:T(8,128)(2,1)S(1)} %collective-permute-done.5, bf16[3456,128]{1,0:T(8,128)(2,1)S(1)} %reshape.28, pred[]{:T(512)S(6)} %eq.4), kind=kLoop, calls=%fused_computation.1 | loop fusion | flops 2654208 | bytes 5308417 | tf_op jit(solution)/shard_map/div | solution.py:297
  (2 shorter events, 0.0 us)
Async XLA Ops:
  2.8 5.0 %collective-permute-start = (bf16[320,256]{1,0:T(8,128)(2,1)}, bf16[320,256]{1,0:T(8,128)(2,1)S(1)}, u32[]{:S(2)}, u32[]{:S(2)}) collective-permute-start(bf16[320,256]{1,0:T(8,128)(2,1)} %get-tuple-element.11), channel_id=1, source_target_pairs={{0,1},{1,0},{2,3},{3,2},{4,5},{5,4},{6,7},{7,6},{8,9},{9,8},{10,11... | collective-permute-start | bytes 491528 | tf_op jit(solution)/shard_map/ppermute | solution.py:20
  4.8 3.0 %collective-permute-start.1 = (bf16[320,256]{1,0:T(8,128)(2,1)}, bf16[320,256]{1,0:T(8,128)(2,1)S(1)}, u32[]{:S(2)}, u32[]{:S(2)}) collective-permute-start(bf16[320,256]{1,0:T(8,128)(2,1)} %get-tuple-element.12), channel_id=1, source_target_pairs={{1,2},{2,1},{3,4},{4,3},{5,6},{6,5},{7,8},{8,7},{9,10},{10,9},{11,... | collective-permute-start | bytes 491528 | tf_op jit(solution)/shard_map/ppermute | solution.py:20
  7.8 0.7 copy-start
  7.8 0.7 copy-start.1
  33.0 6.0 %collective-permute-start.2 = (bf16[3456,128]{1,0:T(8,128)(2,1)}, bf16[3456,128]{1,0:T(8,128)(2,1)S(1)}, u32[]{:S(2)}, u32[]{:S(2)}) collective-permute-start(bf16[3456,128]{1,0:T(8,128)(2,1)} %get-tuple-element.16), channel_id=1, source_target_pairs={{0,64},{64,0},{1,65},{65,1},{2,66},{66,2},{3,67},{67,3},{4,68},{68... | collective-permute-start | bytes 2654216 | tf_op jit(solution)/shard_map/ppermute | solution.py:36
  67.4 5.7 %collective-permute-start.3 = (f32[108,128]{1,0:T(8,128)S(1)}, f32[108,128]{1,0:T(8,128)S(1)}, u32[]{:S(2)}, u32[]{:S(2)}) collective-permute-start(f32[108,128]{1,0:T(8,128)S(1)} %convert_reduce_fusion), channel_id=1, source_target_pairs={{0,8},{8,0},{16,24},{24,16},{1,9},{9,1},{17,25},{25,17},{2,10},{10... | collective-permute-start | bytes 165896 | tf_op jit(solution)/shard_map/ppermute | solution.py:42
  73.1 6.6 %collective-permute-start.4 = (f32[108,128]{1,0:T(8,128)S(1)}, f32[108,128]{1,0:T(8,128)S(1)}, u32[]{:S(2)}, u32[]{:S(2)}) collective-permute-start(f32[108,128]{1,0:T(8,128)S(1)} %add.10), channel_id=1, source_target_pairs={{0,24},{8,16},{16,8},{24,0},{1,25},{9,17},{17,9},{25,1},{2,26},{10... | collective-permute-start | bytes 165896 | tf_op jit(solution)/shard_map/ppermute | solution.py:42
  96.9 14.3 %collective-permute-start.5 = (bf16[3456,128]{1,0:T(8,128)(2,1)S(1)}, bf16[3456,128]{1,0:T(8,128)(2,1)S(1)}, u32[]{:S(2)}, u32[]{:S(2)}) collective-permute-start(bf16[3456,128]{1,0:T(8,128)(2,1)S(1)} %reshape.28), channel_id=1, source_target_pairs={{0,64},{64,0},{1,65},{65,1},{2,66},{66,2},{3,67},{67,3},{4,68},{68... | collective-permute-start | bytes 2654216 | tf_op jit(solution)/shard_map/ppermute | solution.py:45

commit v2 on v1

--- a/solution.py
+++ b/solution.py
@@ -12,6 +12,7 @@
 CODE = 32
 NONE = 4096
 GROUP = 9
+LONG = 9
 
 
 def swapped(x, axis, odd):
@@ -62,17 +63,17 @@
     return jnp.where(ids_ref[...] == place, jnp.ones((), jnp.bfloat16), jnp.zeros((), jnp.bfloat16))
 
 
-def over_offsets(offsets, chans, step):
+def over_offsets(offsets, chans, step, unrolled):
     def group(index, carry):
-        for inner in range(GROUP):
-            k = index * GROUP + inner
+        for inner in range(unrolled):
+            k = index * unrolled + inner
             step(k, pl.ds(pl.multiple_of(k * chans, chans), chans))
         return carry
 
-    lax.fori_loop(0, offsets // GROUP, group, 0)
-
-
-def gather_into(picked_ref, rule_ref, ids_ref, tiles, offsets, start, shift):
+    lax.fori_loop(0, offsets // unrolled, group, 0)
+
+
+def gather_step(picked_ref, rule_ref, ids_ref, tiles, start, shift):
     chans = tiles[0].shape[0]
     sides = [jnp.concatenate([a, b], 0) for a, b in zip(tiles[:-1], tiles[1:])]
 
@@ -84,7 +85,7 @@
             found = jnp.where(half == q, both[:chans], jnp.where(half == q + 1, both[chans:], 0.0))
             picked_ref[at, SPAN * q : SPAN * (q + 1)] = found.astype(jnp.bfloat16)
 
-    over_offsets(offsets, chans, step)
+    return step
 
 
 def side_by_side(w_ref, out_ref, turned):
@@ -93,7 +94,7 @@
         out_ref[:, k * chans : (k + 1) * chans] = w_ref[k].T if turned else w_ref[k]
 
 
-def scatter_to(high_ref, low_ref, rule_ref, ids_ref, sources, w_ref, offsets, start, shift):
+def scatter_step(high_ref, low_ref, rule_ref, ids_ref, sources, start, shift):
     chans = sources[0].shape[0]
     last = len(sources) - 1
 
@@ -121,8 +122,10 @@
                 put(at, q - 1, above + spread[:chans])
             above = spread[-chans:]
 
-    over_offsets(offsets, chans, step)
-    used = SPAN * last
+    return step
+
+
+def through(w_ref, high_ref, low_ref, used):
     total = jnp.dot(w_ref[...], high_ref[:, :used], preferred_element_type=jnp.float32)
     return total + jnp.dot(w_ref[...], low_ref[:, :used], preferred_element_type=jnp.float32)
 
@@ -153,9 +156,12 @@
     high_ref, low_ref, picked_ref, w_ref, before_ref, after_ref, ids_ref,
 ):
     rows, chans = grad_out_ref.shape
-    offsets = mine_ref.shape[0] // chans
+    offsets = w1_ref.shape[0]
+    flat = offsets * chans
     wide = rows + 2 * HALO
     fill_ids(ids_ref)
+    mine_ref[flat:, :] = jnp.zeros((mine_ref.shape[0] - flat, chans), jnp.float32)
+    other_ref[flat:, :] = jnp.zeros((other_ref.shape[0] - flat, chans), jnp.bfloat16)
     is_odd = parity_ref[0] == 1
     before_ref[...] = jnp.where(is_odd, even_ref[...], odd_ref[...])
     after_ref[...] = jnp.where(is_odd, odd_ref[...], even_ref[...])
@@ -173,12 +179,17 @@
         inner = [own_ref[rest, SPAN * p : SPAN * (p + 1)] for p in range(rows // SPAN)]
         return [before_ref[rest, :]] + inner + [after_ref[rest, :]]
 
+    scatter = scatter_step(high_ref, low_ref, rule_ref, ids_ref, tiles(chans), 0, HALO)
+    gather = gather_step(picked_ref, rule_ref, ids_ref, tiles(0), HALO, 0)
+
+    def both(k, at):
+        scatter(k, at)
+        gather(k, at)
+
+    over_offsets(offsets, chans, both, GROUP)
     side_by_side(w2_ref, w_ref, False)
-    grad_act = scatter_to(
-        high_ref, low_ref, rule_ref, ids_ref, tiles(chans), w_ref, offsets, 0, HALO
-    )
+    grad_act = through(w_ref, high_ref, low_ref, wide)
     side_by_side(w1_ref, w_ref, True)
-    gather_into(picked_ref, rule_ref, ids_ref, tiles(0), offsets, HALO, 0)
     hidden = jnp.dot(w_ref[...], picked_ref[...], preferred_element_type=jnp.float32)
     act = (hidden * jax.nn.sigmoid(hidden)).astype(jnp.bfloat16)
     grad_hidden = (grad_act * dsilu(hidden)).astype(jnp.bfloat16)
@@ -190,34 +201,37 @@
 
     @pl.when(core_ref[0] == 0)
     def _():
-        mine_ref[...] = first
+        mine_ref[:flat, :] = first
 
     @pl.when(core_ref[0] != 0)
     def _():
-        other_ref[...] = first.astype(jnp.bfloat16)
+        other_ref[:flat, :] = first.astype(jnp.bfloat16)
 
     act_tiles = [act[:, SPAN * q : SPAN * (q + 1)] for q in range(wide // SPAN)]
-    gather_into(high_ref, rule_ref, ids_ref, act_tiles, offsets, EDGE, EDGE - HALO)
+    gather = gather_step(high_ref, rule_ref, ids_ref, act_tiles, EDGE, EDGE - HALO)
+    over_offsets(offsets, chans, gather, LONG)
     second = jnp.dot(high_ref[:, :rows], grad_out_ref[...], preferred_element_type=jnp.float32)
 
     @pl.when(core_ref[0] != 0)
     def _():
-        mine_ref[...] = second
+        mine_ref[:flat, :] = second
 
     @pl.when(core_ref[0] == 0)
     def _():
-        other_ref[...] = second.astype(jnp.bfloat16)
+        other_ref[:flat, :] = second.astype(jnp.bfloat16)
 
 
 def input_grad_kernel(
     source_ref, rule_ref, w1_ref, grad_out_ref, live_ref, out_ref, high_ref, low_ref, w_ref, ids_ref
 ):
-    rows, _ = grad_out_ref.shape
+    rows, chans = grad_out_ref.shape
     offsets = w1_ref.shape[0]
     fill_ids(ids_ref)
     side_by_side(w1_ref, w_ref, False)
     sources = [source_ref[:, SPAN * q : SPAN * (q + 1)] for q in range(source_ref.shape[1] // SPAN)]
-    total = scatter_to(high_ref, low_ref, rule_ref, ids_ref, sources, w_ref, offsets, HALO, 0)
+    scatter = scatter_step(high_ref, low_ref, rule_ref, ids_ref, sources, HALO, 0)
+    over_offsets(offsets, chans, scatter, LONG)
+    total = through(w_ref, high_ref, low_ref, rows)
     for b in range(rows // BLOCK):
         at = slice(b * BLOCK, (b + 1) * BLOCK)
         added = grad_out_ref[at, :].astype(jnp.float32) + total[:, at].T
@@ -244,6 +258,7 @@
     offsets = w1.shape[0]
     wide = rows + 2 * HALO
     flat = offsets * chans
+    padded = flat + chans
     bf16, f32, i32 = (jnp.bfloat16, jnp.float32, jnp.int32)
     ids = ((SPAN, SPAN), bf16)
     spread = ((flat, wide), bf16)
@@ -261,12 +276,12 @@
         parity,
         scalars=1,
     )
+    odd = swapped(to_odd, BLOCKS, 1)
     even = swapped(to_even, BLOCKS, 0)
-    odd = swapped(to_odd, BLOCKS, 1)
     core = lax.axis_index("core").astype(i32).reshape(1)
     mine, other, grad_hidden, wide_rules = call(
         grads_kernel,
-        [((flat, chans), f32), ((flat, chans), bf16), ((chans, wide), bf16), ((CODE, rows + 2 * EDGE), i32)],
+        [((padded, chans), f32), ((padded, chans), bf16), ((chans, wide), bf16), ((CODE, rows + 2 * EDGE), i32)],
         [spread, spread, spread, beside, ((tall, EDGE), bf16), ((tall, EDGE), bf16), ids],
         own,
         even,
@@ -294,7 +309,7 @@
     kern_one, kern_two = reduce_everywhere(mine, other)
     voxel_total = rows * lax.axis_size(REGIONS) * lax.axis_size(BLOCKS)
     scale = jnp.sqrt(jnp.float32(voxel_total))
-    return (grad_in, kern_one.reshape(w1.shape) / scale, kern_two.reshape(w1.shape) / scale)
+    return (grad_in, kern_one[:flat].reshape(w1.shape) / scale, kern_two[:flat].reshape(w1.shape) / scale)
 
 
 def solution(mesh):

time: 114 us -> 111 us (0.974)
  Pallas kernels: 35.9 us -> 34 us
    pallas_call x3, Pallas kernels: 35.9 us -> 34 us  [call(): pl.pallas_call(kernel, out_shape=shapes, in_specs=[vmem] * (len(args) - s...]
where the time goes in v2:
time: 111 us
  blocking collectives  43.3 us (39%)
  Pallas kernels  34 us (31%)
  starting transfers between devices  19.9 us (18%)
  waiting for transfers between devices  8.28 us (7%)
  other arithmetic  4.02 us (4%)
    pallas_call x3, Pallas kernels, call(): pl.pallas_call(kernel, out_shape=shapes, in_specs=[vmem] * (len(args) - s...  34 us
    all_to_all x1, blocking collectives, reduce_everywhere(): parts = lax.all_to_all(parts, PLANE, 0, 0, tiled=True)  26.4 us
    all_to_all x1, blocking collectives, reduce_everywhere(): parts = lax.all_to_all(parts, PLANE, 0, 0, tiled=True).reshape(-1, lanes)  17 us
    ppermute x2, starting transfers between devices, reduce_everywhere(): lax.ppermute(own, 'z_hi', [(i, i ^ flip) for i in range(lax.axis_size('z_...  8.62 us
    ppermute x1, starting transfers between devices, reduce_everywhere(): other = lax.ppermute(parts, 'core', SWAP)  4.92 us
    ppermute x1, starting transfers between devices, reduce_everywhere(): own = own + lax.ppermute(other, 'core', SWAP).astype(jnp.float32)  3.72 us
    ppermute x2, waiting for transfers between devices, reduce_everywhere(): lax.ppermute(own, 'z_hi', [(i, i ^ flip) for i in range(lax.axis_size('z_...  3.65 us
    ppermute x2, starting transfers between devices, swapped(): return lax.ppermute(x, axis, [(i, j) for i, j in pairs if 0 <= j < length])  2.69 us
  transfers between devices with their start and end apart: 6, of which 4 were waited for; matrix products, arithmetic and copies ran while one was open for 0% of the time, Pallas kernels for 8%

profile of v2, /device:TPU:1, one launch (start us, length us, event | category | flops | bytes accessed | tf_op | source)
XLA Modules:
  0.0 111.0 jit_solution(8095446801619956448)
XLA Ops:
  0.6 2.1 %shard_map.85 = (bf16[320,768]{1,0:T(8,128)(2,1)}, bf16[320,256]{1,0:T(8,128)(2,1)}, bf16[320,256]{1,0:T(8,128)(2,1)}) custom-call(bf16[768,128]{1,0:T(8,128)(2,1)} %feat_ref.1, bf16[768,128]{1,0:T(8,128)(2,1)} %grad_out_ref.3, s32[27,768]{1,0:T(8,128)} %rule_ref.1, s32[1]{0:T(128)} %bitcast.odd_ref.parity_ref), custom_call_target="tpu_custom_call" | custom-call | bytes 1295364 | tf_op jit(solution)/shard_map/pallas_call | solution.py:246
  2.8 2.0 %collective-permute-start = (bf16[320,256]{1,0:T(8,128)(2,1)}, bf16[320,256]{1,0:T(8,128)(2,1)S(1)}, u32[]{:S(2)}, u32[]{:S(2)}) collective-permute-start(bf16[320,256]{1,0:T(8,128)(2,1)} %get-tuple-element.11), channel_id=1, source_target_pairs={{0,1},{1,0},{2,3},{3,2},{4,5},{5,4},{6,7},{7,6},{8,9},{9,8},{10,11... | collective-permute-start | bytes 491528 | tf_op jit(solution)/shard_map/ppermute | solution.py:21
  4.8 0.7 collective-permute-start.1
  5.5 2.3 %collective-permute-done.even_ref = bf16[320,256]{1,0:T(8,128)(2,1)S(1)} collective-permute-done((bf16[320,256]{1,0:T(8,128)(2,1)}, bf16[320,256]{1,0:T(8,128)(2,1)S(1)}, u32[]{:S(2)}, u32[]{:S(2)}) %collective-permute-start) | collective-permute-done | bytes 163872 | tf_op jit(solution)/shard_map/ppermute | solution.py:21
  7.8 0.0 copy-start
  7.8 0.0 collective-permute-done.1.odd_ref
  7.8 0.0 copy-start.1
  7.8 0.7 copy-done
  8.5 0.0 copy-done.1
  8.5 22.6 %shard_map.86 = (f32[3584,128]{1,0:T(8,128)}, bf16[3584,128]{1,0:T(8,128)(2,1)}, bf16[128,1024]{1,0:T(8,128)(2,1)}, s32[32,1280]{1,0:T(8,128)}) custom-call(bf16[320,768]{1,0:T(8,128)(2,1)} %get-tuple-element.10.own_ref, bf16[320,256]{1,0:T(8,128)(2,1)} %copy-done, bf16[320,256]{1,0:T(8,128)(2,1)} %copy-done.1, bf16[768,128]{1,0:T(8,128)(2,1)} %grad_out_ref.3, ...), custom_call_target="tpu_custom_call" | custom-call | flops 16307453952 | bytes 5963784 | tf_op jit(solution)/shard_map/pallas_call | solution.py:246
  31.1 3.7 %collective-permute-start.2 = (bf16[3584,128]{1,0:T(8,128)(2,1)}, bf16[3584,128]{1,0:T(8,128)(2,1)S(1)}, u32[]{:S(2)}, u32[]{:S(2)}) collective-permute-start(bf16[3584,128]{1,0:T(8,128)(2,1)} %get-tuple-element.16), channel_id=1, source_target_pairs={{0,64},{64,0},{1,65},{65,1},{2,66},{66,2},{3,67},{67,3},{4,68},{68... | collective-permute-start | bytes 2752520 | tf_op jit(solution)/shard_map/ppermute | solution.py:37
  34.8 2.3 %collective-permute-done.2 = bf16[3584,128]{1,0:T(8,128)(2,1)S(1)} collective-permute-done((bf16[3584,128]{1,0:T(8,128)(2,1)}, bf16[3584,128]{1,0:T(8,128)(2,1)S(1)}, u32[]{:S(2)}, u32[]{:S(2)}) %collective-permute-start.2) | collective-permute-done | bytes 917536 | tf_op jit(solution)/shard_map/ppermute | solution.py:37
  37.1 1.7 %add_convert_fusion = bf16[3584,128]{1,0:T(8,128)(2,1)S(1)} fusion(f32[3584,128]{1,0:T(8,128)} %get-tuple-element.15, bf16[3584,128]{1,0:T(8,128)(2,1)S(1)} %collective-permute-done.2), kind=kLoop, calls=%fused_computation.1 | loop fusion | flops 1376256 | bytes 3670016 | tf_op jit(solution)/shard_map/convert_element_type | solution.py:39
  38.8 26.4 %all_to_all.10 = bf16[32,112,128]{2,1,0:T(8,128)(2,1)S(1)} all-to-all(bf16[32,112,128]{2,1,0:T(8,128)(2,1)S(1)} %bitcast.6), channel_id=1, replica_groups=mesh['yh'=2,'core'=2,'yl'=2,'z_hi'=4,'z_lo'=2,'x'=4] {'yh','yl','z_lo','x'}, dimensions={0} | all-to-all | bytes 1835008 | tf_op jit(solution)/shard_map/all_to_all | solution.py:40
  65.2 0.1 convert_reduce_fusion
  65.3 3.6 %collective-permute-start.3 = (f32[112,128]{1,0:T(8,128)S(1)}, f32[112,128]{1,0:T(8,128)S(1)}, u32[]{:S(2)}, u32[]{:S(2)}) collective-permute-start(f32[112,128]{1,0:T(8,128)S(1)} %convert_reduce_fusion), channel_id=1, source_target_pairs={{0,8},{8,0},{16,24},{24,16},{1,9},{9,1},{17,25},{25,17},{2,10},{10... | collective-permute-start | bytes 172040 | tf_op jit(solution)/shard_map/ppermute | solution.py:43
  68.9 2.0 %collective-permute-done.3 = f32[112,128]{1,0:T(8,128)S(1)} collective-permute-done((f32[112,128]{1,0:T(8,128)S(1)}, f32[112,128]{1,0:T(8,128)S(1)}, u32[]{:S(2)}, u32[]{:S(2)}) %collective-permute-start.3) | collective-permute-done | bytes 57376 | tf_op jit(solution)/shard_map/ppermute | solution.py:43
  71.0 5.0 %collective-permute-start.4 = (f32[112,128]{1,0:T(8,128)S(1)}, f32[112,128]{1,0:T(8,128)S(1)}, u32[]{:S(2)}, u32[]{:S(2)}) collective-permute-start(f32[112,128]{1,0:T(8,128)S(1)} %add.10), channel_id=1, source_target_pairs={{0,24},{8,16},{16,8},{24,0},{1,25},{9,17},{17,9},{25,1},{2,26},{10... | collective-permute-start | bytes 172040 | tf_op jit(solution)/shard_map/ppermute | solution.py:43
  76.0 1.6 %collective-permute-done.4 = f32[112,128]{1,0:T(8,128)S(1)} collective-permute-done((f32[112,128]{1,0:T(8,128)S(1)}, f32[112,128]{1,0:T(8,128)S(1)}, u32[]{:S(2)}, u32[]{:S(2)}) %collective-permute-start.4) | collective-permute-done | bytes 57376 | tf_op jit(solution)/shard_map/ppermute | solution.py:43
  77.6 0.1 broadcast_in_dim.2
  77.7 17.0 %all_to_all.11 = bf16[32,112,128]{2,1,0:T(8,128)(2,1)S(1)} all-to-all(bf16[32,112,128]{2,1,0:T(8,128)(2,1)S(1)} %broadcast_in_dim.2), channel_id=1, replica_groups=mesh['yh'=2,'core'=2,'yl'=2,'z_hi'=4,'z_lo'=2,'x'=4] {'yh','yl','z_lo','x'}, dimensions={0} | all-to-all | bytes 1835008 | tf_op jit(solution)/shard_map/all_to_all | solution.py:45
  94.7 4.9 %collective-permute-start.5 = (bf16[3584,128]{1,0:T(8,128)(2,1)S(1)}, bf16[3584,128]{1,0:T(8,128)(2,1)S(1)}, u32[]{:S(2)}, u32[]{:S(2)}) collective-permute-start(bf16[3584,128]{1,0:T(8,128)(2,1)S(1)} %bitcast.7), channel_id=1, source_target_pairs={{0,64},{64,0},{1,65},{65,1},{2,66},{66,2},{3,67},{67,3},{4,68},{68... | collective-permute-start | bytes 2752520 | tf_op jit(solution)/shard_map/ppermute | solution.py:46
  99.6 9.2 %shard_map.87 = bf16[768,128]{1,0:T(8,128)(2,1)} custom-call(bf16[128,1024]{1,0:T(8,128)(2,1)} %get-tuple-element.13.source_ref, s32[32,1280]{1,0:T(8,128)} %get-tuple-element.14.rule_ref, bf16[27,128,128]{2,1,0:T(8,128)(2,1)} %w1_ref.3, bf16[768,128]{1,0:T(8,128)(2,1)} %grad_out_ref.3, s32[6]{0:T(128)} %live_ref.1), custom_call_target="tpu_custom_call" | custom-call | flops 5435817984 | bytes 1703960 | tf_op jit(solution)/shard_map/pallas_call | solution.py:246
  108.9 0.0 collective-permute-done.5
  108.9 2.1 %convert_multiply_fusion = (f32[3456,128]{1,0:T(8,128)}, f32[3456,128]{1,0:T(8,128)}) fusion(pred[]{:T(512)S(6)} %eq.4, bf16[3584,128]{1,0:T(8,128)(2,1)S(1)} %collective-permute-done.5, bf16[3584,128]{1,0:T(8,128)(2,1)S(1)} %bitcast.8), kind=kLoop, calls=%fused_computation.2 | loop fusion | flops 2654208 | bytes 5308417 | tf_op jit(solution)/shard_map/div | solution.py:312
  (2 shorter events, 0.0 us)
Async XLA Ops:
  2.8 5.0 %collective-permute-start = (bf16[320,256]{1,0:T(8,128)(2,1)}, bf16[320,256]{1,0:T(8,128)(2,1)S(1)}, u32[]{:S(2)}, u32[]{:S(2)}) collective-permute-start(bf16[320,256]{1,0:T(8,128)(2,1)} %get-tuple-element.11), channel_id=1, source_target_pairs={{0,1},{1,0},{2,3},{3,2},{4,5},{5,4},{6,7},{7,6},{8,9},{9,8},{10,11... | collective-permute-start | bytes 491528 | tf_op jit(solution)/shard_map/ppermute | solution.py:21
  4.8 3.0 %collective-permute-start.1 = (bf16[320,256]{1,0:T(8,128)(2,1)}, bf16[320,256]{1,0:T(8,128)(2,1)S(1)}, u32[]{:S(2)}, u32[]{:S(2)}) collective-permute-start(bf16[320,256]{1,0:T(8,128)(2,1)} %get-tuple-element.12), channel_id=1, source_target_pairs={{1,2},{2,1},{3,4},{4,3},{5,6},{6,5},{7,8},{8,7},{9,10},{10,9},{11,... | collective-permute-start | bytes 491528 | tf_op jit(solution)/shard_map/ppermute | solution.py:21
  7.8 0.7 copy-start
  7.8 0.7 copy-start.1
  31.1 6.0 %collective-permute-start.2 = (bf16[3584,128]{1,0:T(8,128)(2,1)}, bf16[3584,128]{1,0:T(8,128)(2,1)S(1)}, u32[]{:S(2)}, u32[]{:S(2)}) collective-permute-start(bf16[3584,128]{1,0:T(8,128)(2,1)} %get-tuple-element.16), channel_id=1, source_target_pairs={{0,64},{64,0},{1,65},{65,1},{2,66},{66,2},{3,67},{67,3},{4,68},{68... | collective-permute-start | bytes 2752520 | tf_op jit(solution)/shard_map/ppermute | solution.py:37
  65.3 5.7 %collective-permute-start.3 = (f32[112,128]{1,0:T(8,128)S(1)}, f32[112,128]{1,0:T(8,128)S(1)}, u32[]{:S(2)}, u32[]{:S(2)}) collective-permute-start(f32[112,128]{1,0:T(8,128)S(1)} %convert_reduce_fusion), channel_id=1, source_target_pairs={{0,8},{8,0},{16,24},{24,16},{1,9},{9,1},{17,25},{25,17},{2,10},{10... | collective-permute-start | bytes 172040 | tf_op jit(solution)/shard_map/ppermute | solution.py:43
  71.0 6.6 %collective-permute-start.4 = (f32[112,128]{1,0:T(8,128)S(1)}, f32[112,128]{1,0:T(8,128)S(1)}, u32[]{:S(2)}, u32[]{:S(2)}) collective-permute-start(f32[112,128]{1,0:T(8,128)S(1)} %add.10), channel_id=1, source_target_pairs={{0,24},{8,16},{16,8},{24,0},{1,25},{9,17},{17,9},{25,1},{2,26},{10... | collective-permute-start | bytes 172040 | tf_op jit(solution)/shard_map/ppermute | solution.py:43
  94.7 14.2 %collective-permute-start.5 = (bf16[3584,128]{1,0:T(8,128)(2,1)S(1)}, bf16[3584,128]{1,0:T(8,128)(2,1)S(1)}, u32[]{:S(2)}, u32[]{:S(2)}) collective-permute-start(bf16[3584,128]{1,0:T(8,128)(2,1)S(1)} %bitcast.7), channel_id=1, source_target_pairs={{0,64},{64,0},{1,65},{65,1},{2,66},{66,2},{3,67},{67,3},{4,68},{68... | collective-permute-start | bytes 2752520 | tf_op jit(solution)/shard_map/ppermute | solution.py:46

commit v3 on v2

--- a/solution.py
+++ b/solution.py
@@ -73,17 +73,18 @@
     lax.fori_loop(0, offsets // unrolled, group, 0)
 
 
-def gather_step(picked_ref, rule_ref, ids_ref, tiles, start, shift):
+def gather_step(picked_ref, rule_ref, ids_ref, tiles, start, shift, groups=None):
     chans = tiles[0].shape[0]
-    sides = [jnp.concatenate([a, b], 0) for a, b in zip(tiles[:-1], tiles[1:])]
+    groups = range(len(tiles) - 1) if groups is None else groups
+    sides = [jnp.concatenate([tiles[q], tiles[q + 1]], 0) for q in groups]
 
     def step(k, at):
-        for q, side in enumerate(sides):
+        for slot, (q, side) in enumerate(zip(groups, sides)):
             entries = rule_ref[pl.ds(k, 1), start + SPAN * q : start + SPAN * (q + 1)] - shift
             both = jnp.dot(side, one_hot(ids_ref, entries), preferred_element_type=jnp.float32)
             half = lax.shift_right_arithmetic(entries, 8)
             found = jnp.where(half == q, both[:chans], jnp.where(half == q + 1, both[chans:], 0.0))
-            picked_ref[at, SPAN * q : SPAN * (q + 1)] = found.astype(jnp.bfloat16)
+            picked_ref[at, SPAN * slot : SPAN * (slot + 1)] = found.astype(jnp.bfloat16)
 
     return step
 
@@ -150,15 +151,35 @@
     to_odd_ref[...] = jnp.where(odd, last, first)
 
 
+def wide_entries(piece, chans, base):
+    coarse = piece[2 * chans : 2 * chans + CODE, :].astype(jnp.float32)
+    fine = piece[2 * chans + CODE :, :].astype(jnp.float32)
+    code = (coarse * 32.0 + fine).astype(jnp.int32)
+    return jnp.where(code == 0, NONE, code - 1 + base)
+
+
+def early_kernel(own_ref, picked_ref, rule_ref, ids_ref):
+    flat, _ = picked_ref.shape
+    rows = own_ref.shape[1]
+    chans = (own_ref.shape[0] - 2 * CODE) // 2
+    fill_ids(ids_ref)
+    rule_ref[...] = wide_entries(own_ref, chans, -HALO)
+    inner = [own_ref[:chans, SPAN * p : SPAN * (p + 1)] for p in range(rows // SPAN)]
+    gather = gather_step(picked_ref, rule_ref, ids_ref, inner, HALO, 0)
+    over_offsets(flat // chans, chans, gather, LONG)
+
+
 def grads_kernel(
-    own_ref, even_ref, odd_ref, grad_out_ref, w1_ref, w2_ref, core_ref, parity_ref,
+    own_ref, even_ref, odd_ref, grad_out_ref, w1_ref, w2_ref, early_ref, core_ref, parity_ref,
     mine_ref, other_ref, source_ref, rule_ref,
-    high_ref, low_ref, picked_ref, w_ref, before_ref, after_ref, ids_ref,
+    high_ref, low_ref, edge_ref, middle_ref, w_ref, before_ref, after_ref, ids_ref, sem,
 ):
     rows, chans = grad_out_ref.shape
     offsets = w1_ref.shape[0]
     flat = offsets * chans
     wide = rows + 2 * HALO
+    arriving = pltpu.make_async_copy(early_ref, middle_ref, sem)
+    arriving.start()
     fill_ids(ids_ref)
     mine_ref[flat:, :] = jnp.zeros((mine_ref.shape[0] - flat, chans), jnp.float32)
     other_ref[flat:, :] = jnp.zeros((other_ref.shape[0] - flat, chans), jnp.bfloat16)
@@ -168,11 +189,9 @@
     pieces = ((before_ref, -HALO - rows + EDGE), (own_ref, EDGE - HALO), (after_ref, EDGE - HALO + rows))
     column = 0
     for piece, base in pieces:
-        coarse = piece[2 * chans : 2 * chans + CODE, :].astype(jnp.float32)
-        fine = piece[2 * chans + CODE :, :].astype(jnp.float32)
-        code = (coarse * 32.0 + fine).astype(jnp.int32)
-        rule_ref[:, column : column + code.shape[1]] = jnp.where(code == 0, NONE, code - 1 + base)
-        column += code.shape[1]
+        entries = wide_entries(piece, chans, base)
+        rule_ref[:, column : column + entries.shape[1]] = entries
+        column += entries.shape[1]
 
     def tiles(top):
         rest = slice(top, top + chans)
@@ -180,7 +199,8 @@
         return [before_ref[rest, :]] + inner + [after_ref[rest, :]]
 
     scatter = scatter_step(high_ref, low_ref, rule_ref, ids_ref, tiles(chans), 0, HALO)
-    gather = gather_step(picked_ref, rule_ref, ids_ref, tiles(0), HALO, 0)
+    ends = (0, wide // SPAN - 1)
+    gather = gather_step(edge_ref, rule_ref, ids_ref, tiles(0), HALO, 0, ends)
 
     def both(k, at):
         scatter(k, at)
@@ -190,14 +210,18 @@
     side_by_side(w2_ref, w_ref, False)
     grad_act = through(w_ref, high_ref, low_ref, wide)
     side_by_side(w1_ref, w_ref, True)
-    hidden = jnp.dot(w_ref[...], picked_ref[...], preferred_element_type=jnp.float32)
+    arriving.wait()
+    ended = jnp.dot(w_ref[...], edge_ref[...], preferred_element_type=jnp.float32)
+    middle = jnp.dot(w_ref[...], middle_ref[...], preferred_element_type=jnp.float32)
+    hidden = jnp.concatenate([ended[:, :SPAN], middle, ended[:, SPAN:]], 1)
     act = (hidden * jax.nn.sigmoid(hidden)).astype(jnp.bfloat16)
     grad_hidden = (grad_act * dsilu(hidden)).astype(jnp.bfloat16)
     source_ref[...] = grad_hidden
-    inside = slice(HALO, HALO + rows)
+    outer = jnp.concatenate([grad_hidden[:, HALO:SPAN], grad_hidden[:, wide - SPAN : wide - HALO]], 1)
+    across = (((1,), (1,)), ((), ()))
     first = lax.dot_general(
-        picked_ref[:, inside], grad_hidden[:, inside], (((1,), (1,)), ((), ())), preferred_element_type=jnp.float32
-    )
+        middle_ref[...], grad_hidden[:, SPAN : wide - SPAN], across, preferred_element_type=jnp.float32
+    ) + lax.dot_general(edge_ref[:, HALO : SPAN + HALO], outer, across, preferred_element_type=jnp.float32)
 
     @pl.when(core_ref[0] == 0)
     def _():
@@ -238,17 +262,18 @@
         out_ref[at, :] = (live_ref[b].astype(jnp.float32) * added).astype(jnp.bfloat16)
 
 
-def call(kernel, outs, scratch, *args, scalars=0, flops=0):
+def call(kernel, outs, scratch, *args, scalars=0, held=0, flops=0):
     vmem = pl.BlockSpec(memory_space=pltpu.VMEM)
+    hbm = pl.BlockSpec(memory_space=pl.ANY)
     smem = pl.BlockSpec(memory_space=pltpu.SMEM)
     shapes = [jax.ShapeDtypeStruct(shape, dtype) for shape, dtype in outs]
     moved = sum(x.size * x.dtype.itemsize for x in (*args, *shapes))
     return pl.pallas_call(
         kernel,
         out_shape=shapes,
-        in_specs=[vmem] * (len(args) - scalars) + [smem] * scalars,
+        in_specs=[vmem] * (len(args) - scalars - held) + [hbm] * held + [smem] * scalars,
         out_specs=[vmem] * len(outs),
-        scratch_shapes=[pltpu.VMEM(shape, dtype) for shape, dtype in scratch],
+        scratch_shapes=[pltpu.VMEM(*kind) for kind in scratch] + [pltpu.SemaphoreType.DMA] * held,
         cost_estimate=pl.CostEstimate(flops=flops, bytes_accessed=moved, transcendentals=0),
     )(*args)
 
@@ -262,6 +287,7 @@
     bf16, f32, i32 = (jnp.bfloat16, jnp.float32, jnp.int32)
     ids = ((SPAN, SPAN), bf16)
     spread = ((flat, wide), bf16)
+    half = ((flat, wide - 2 * SPAN), bf16)
     beside = ((chans, flat), bf16)
     tall = 2 * chans + 2 * CODE
     one_pass = 2 * offsets * rows * SPAN * SPAN
@@ -276,22 +302,25 @@
         parity,
         scalars=1,
     )
+    even = swapped(to_even, BLOCKS, 0)
     odd = swapped(to_odd, BLOCKS, 1)
-    even = swapped(to_even, BLOCKS, 0)
+    (early,) = call(early_kernel, [((flat, wide - 2 * SPAN), bf16)], [((CODE, rows), i32), ids], own, flops=one_pass)
     core = lax.axis_index("core").astype(i32).reshape(1)
     mine, other, grad_hidden, wide_rules = call(
         grads_kernel,
         [((padded, chans), f32), ((padded, chans), bf16), ((chans, wide), bf16), ((CODE, rows + 2 * EDGE), i32)],
-        [spread, spread, spread, beside, ((tall, EDGE), bf16), ((tall, EDGE), bf16), ids],
+        [spread, spread, half, half, beside, ((tall, EDGE), bf16), ((tall, EDGE), bf16), ids],
         own,
         even,
         odd,
         grad_out,
         w1,
         w2,
+        early,
         core,
         parity,
         scalars=2,
+        held=1,
         flops=6 * one_pass,
     )
     (grad_in,) = call(

time: 111 us -> 110 us (level)
  Pallas kernels: 34 us -> 38.1 us
  starting transfers between devices: 19.9 us -> 16.2 us
  waiting for transfers between devices: 8.28 us -> 6.13 us
    pallas_call x3 -> x4, Pallas kernels: 34 us -> 38.1 us  [call(): pl.pallas_call(kernel, out_shape=shapes, in_specs=[vmem] * (len(args) - s...]
    ppermute x2, waiting for transfers between devices: 2.31 us -> 0.01 us  [swapped(): return lax.ppermute(x, axis, [(i, j) for i, j in pairs if 0 <= j < length])]
    ppermute x1, starting transfers between devices: 3.72 us -> 1.44 us  [reduce_everywhere(): own = own + lax.ppermute(other, 'core', SWAP).astype(jnp.float32)]
    ppermute x2, starting transfers between devices: 8.62 us -> 7.11 us  [reduce_everywhere(): lax.ppermute(own, 'z_hi', [(i, i ^ flip) for i in range(lax.axis_size('z_...]
  transfers between devices with their start and end apart: 6 -> 6, of which waited for: 4 -> 3; matrix products, arithmetic and copies ran while one was open for 0% -> 0% of each run, Pallas kernels for 8% -> 13%
where the time goes in v3:
time: 110 us
  blocking collectives  44.1 us (40%)
  Pallas kernels  38.1 us (35%)
  starting transfers between devices  16.2 us (15%)
  waiting for transfers between devices  6.13 us (6%)
  other arithmetic  4.02 us (4%)
    pallas_call x4, Pallas kernels, call(): pl.pallas_call(kernel, out_shape=shapes, in_specs=[vmem] * (len(args) - s...  38.1 us
    all_to_all x1, blocking collectives, reduce_everywhere(): parts = lax.all_to_all(parts, PLANE, 0, 0, tiled=True)  27.2 us
    all_to_all x1, blocking collectives, reduce_everywhere(): parts = lax.all_to_all(parts, PLANE, 0, 0, tiled=True).reshape(-1, lanes)  17 us
    ppermute x2, starting transfers between devices, reduce_everywhere(): lax.ppermute(own, 'z_hi', [(i, i ^ flip) for i in range(lax.axis_size('z_...  7.11 us
    ppermute x1, starting transfers between devices, reduce_everywhere(): other = lax.ppermute(parts, 'core', SWAP)  4.92 us
    ppermute x2, waiting for transfers between devices, reduce_everywhere(): lax.ppermute(own, 'z_hi', [(i, i ^ flip) for i in range(lax.axis_size('z_...  3.81 us
    ppermute x2, starting transfers between devices, swapped(): return lax.ppermute(x, axis, [(i, j) for i, j in pairs if 0 <= j < length])  2.69 us
    ppermute x1, waiting for transfers between devices, reduce_everywhere(): own = own + lax.ppermute(other, 'core', SWAP).astype(jnp.float32)  2.31 us
  transfers between devices with their start and end apart: 6, of which 3 were waited for; matrix products, arithmetic and copies ran while one was open for 0% of the time, Pallas kernels for 13%

profile of v3, /device:TPU:1, one launch (start us, length us, event | category | flops | bytes accessed | tf_op | source)
XLA Modules:
  0.0 110.1 jit_solution(5188752993039015267)
XLA Ops:
  0.6 2.1 %shard_map.85 = (bf16[320,768]{1,0:T(8,128)(2,1)}, bf16[320,256]{1,0:T(8,128)(2,1)}, bf16[320,256]{1,0:T(8,128)(2,1)}) custom-call(bf16[768,128]{1,0:T(8,128)(2,1)} %feat_ref.1, bf16[768,128]{1,0:T(8,128)(2,1)} %grad_out_ref.3, s32[27,768]{1,0:T(8,128)} %rule_ref.1, s32[1]{0:T(128)} %bitcast.odd_ref.parity_ref), custom_call_target="tpu_custom_call" | custom-call | bytes 1295364 | tf_op jit(solution)/shard_map/pallas_call | solution.py:271
  2.8 2.0 %collective-permute-start = (bf16[320,256]{1,0:T(8,128)(2,1)}, bf16[320,256]{1,0:T(8,128)(2,1)S(1)}, u32[]{:S(2)}, u32[]{:S(2)}) collective-permute-start(bf16[320,256]{1,0:T(8,128)(2,1)} %get-tuple-element.11), channel_id=1, source_target_pairs={{0,1},{1,0},{2,3},{3,2},{4,5},{5,4},{6,7},{7,6},{8,9},{9,8},{10,11... | collective-permute-start | bytes 491528 | tf_op jit(solution)/shard_map/ppermute | solution.py:21
  4.8 0.7 collective-permute-start.1
  5.5 5.4 %shard_map.86.early_ref = bf16[3456,512]{1,0:T(8,128)(2,1)} custom-call(bf16[320,768]{1,0:T(8,128)(2,1)} %get-tuple-element.10.own_ref), custom_call_target="tpu_custom_call" | custom-call | flops 2717908992 | bytes 4030464 | tf_op jit(solution)/shard_map/pallas_call | solution.py:271
  10.9 0.0 collective-permute-done.even_ref
  10.9 0.0 copy-start
  10.9 0.0 collective-permute-done.1.odd_ref
  10.9 0.0 copy-start.1
  10.9 0.6 copy-done
  11.5 0.1 copy-done.1
  11.6 21.3 %shard_map.87 = (f32[3584,128]{1,0:T(8,128)}, bf16[3584,128]{1,0:T(8,128)(2,1)}, bf16[128,1024]{1,0:T(8,128)(2,1)}, s32[32,1280]{1,0:T(8,128)}) custom-call(bf16[320,768]{1,0:T(8,128)(2,1)} %get-tuple-element.10.own_ref, bf16[320,256]{1,0:T(8,128)(2,1)} %copy-done, bf16[320,256]{1,0:T(8,128)(2,1)} %copy-done.1, bf16[768,128]{1,0:T(8,128)(2,1)} %grad_out_ref.3, ...), custom_call_target="tpu_custom_call" | custom-call | flops 16307453952 | bytes 9502728 | tf_op jit(solution)/shard_map/pallas_call | solution.py:271
  32.9 1.4 %collective-permute-start.2 = (bf16[3584,128]{1,0:T(8,128)(2,1)}, bf16[3584,128]{1,0:T(8,128)(2,1)S(1)}, u32[]{:S(2)}, u32[]{:S(2)}) collective-permute-start(bf16[3584,128]{1,0:T(8,128)(2,1)} %get-tuple-element.16), channel_id=1, source_target_pairs={{0,64},{64,0},{1,65},{65,1},{2,66},{66,2},{3,67},{67,3},{4,68},{68... | collective-permute-start | bytes 2752520 | tf_op jit(solution)/shard_map/ppermute | solution.py:37
  34.4 2.3 %collective-permute-done.2 = bf16[3584,128]{1,0:T(8,128)(2,1)S(1)} collective-permute-done((bf16[3584,128]{1,0:T(8,128)(2,1)}, bf16[3584,128]{1,0:T(8,128)(2,1)S(1)}, u32[]{:S(2)}, u32[]{:S(2)}) %collective-permute-start.2) | collective-permute-done | bytes 917536 | tf_op jit(solution)/shard_map/ppermute | solution.py:37
  36.7 1.7 %add_convert_fusion = bf16[3584,128]{1,0:T(8,128)(2,1)S(1)} fusion(f32[3584,128]{1,0:T(8,128)} %get-tuple-element.15, bf16[3584,128]{1,0:T(8,128)(2,1)S(1)} %collective-permute-done.2), kind=kLoop, calls=%fused_computation.1 | loop fusion | flops 1376256 | bytes 3670016 | tf_op jit(solution)/shard_map/convert_element_type | solution.py:39
  38.4 27.2 %all_to_all.10 = bf16[32,112,128]{2,1,0:T(8,128)(2,1)S(1)} all-to-all(bf16[32,112,128]{2,1,0:T(8,128)(2,1)S(1)} %bitcast.6), channel_id=1, replica_groups=mesh['yh'=2,'core'=2,'yl'=2,'z_hi'=4,'z_lo'=2,'x'=4] {'yh','yl','z_lo','x'}, dimensions={0} | all-to-all | bytes 1835008 | tf_op jit(solution)/shard_map/all_to_all | solution.py:40
  65.6 0.1 convert_reduce_fusion
  65.7 2.3 %collective-permute-start.3 = (f32[112,128]{1,0:T(8,128)S(1)}, f32[112,128]{1,0:T(8,128)S(1)}, u32[]{:S(2)}, u32[]{:S(2)}) collective-permute-start(f32[112,128]{1,0:T(8,128)S(1)} %convert_reduce_fusion), channel_id=1, source_target_pairs={{0,8},{8,0},{16,24},{24,16},{1,9},{9,1},{17,25},{25,17},{2,10},{10... | collective-permute-start | bytes 172040 | tf_op jit(solution)/shard_map/ppermute | solution.py:43
  68.0 2.2 %collective-permute-done.3 = f32[112,128]{1,0:T(8,128)S(1)} collective-permute-done((f32[112,128]{1,0:T(8,128)S(1)}, f32[112,128]{1,0:T(8,128)S(1)}, u32[]{:S(2)}, u32[]{:S(2)}) %collective-permute-start.3) | collective-permute-done | bytes 57376 | tf_op jit(solution)/shard_map/ppermute | solution.py:43
  70.2 4.8 %collective-permute-start.4 = (f32[112,128]{1,0:T(8,128)S(1)}, f32[112,128]{1,0:T(8,128)S(1)}, u32[]{:S(2)}, u32[]{:S(2)}) collective-permute-start(f32[112,128]{1,0:T(8,128)S(1)} %add.10), channel_id=1, source_target_pairs={{0,24},{8,16},{16,8},{24,0},{1,25},{9,17},{17,9},{25,1},{2,26},{10... | collective-permute-start | bytes 172040 | tf_op jit(solution)/shard_map/ppermute | solution.py:43
  75.1 1.6 %collective-permute-done.4 = f32[112,128]{1,0:T(8,128)S(1)} collective-permute-done((f32[112,128]{1,0:T(8,128)S(1)}, f32[112,128]{1,0:T(8,128)S(1)}, u32[]{:S(2)}, u32[]{:S(2)}) %collective-permute-start.4) | collective-permute-done | bytes 57376 | tf_op jit(solution)/shard_map/ppermute | solution.py:43
  76.7 0.1 broadcast_in_dim.2
  76.8 17.0 %all_to_all.11 = bf16[32,112,128]{2,1,0:T(8,128)(2,1)S(1)} all-to-all(bf16[32,112,128]{2,1,0:T(8,128)(2,1)S(1)} %broadcast_in_dim.2), channel_id=1, replica_groups=mesh['yh'=2,'core'=2,'yl'=2,'z_hi'=4,'z_lo'=2,'x'=4] {'yh','yl','z_lo','x'}, dimensions={0} | all-to-all | bytes 1835008 | tf_op jit(solution)/shard_map/all_to_all | solution.py:45
  93.8 4.9 %collective-permute-start.5 = (bf16[3584,128]{1,0:T(8,128)(2,1)S(1)}, bf16[3584,128]{1,0:T(8,128)(2,1)S(1)}, u32[]{:S(2)}, u32[]{:S(2)}) collective-permute-start(bf16[3584,128]{1,0:T(8,128)(2,1)S(1)} %bitcast.7), channel_id=1, source_target_pairs={{0,64},{64,0},{1,65},{65,1},{2,66},{66,2},{3,67},{67,3},{4,68},{68... | collective-permute-start | bytes 2752520 | tf_op jit(solution)/shard_map/ppermute | solution.py:46
  98.7 9.2 %shard_map.88 = bf16[768,128]{1,0:T(8,128)(2,1)} custom-call(bf16[128,1024]{1,0:T(8,128)(2,1)} %get-tuple-element.13.source_ref, s32[32,1280]{1,0:T(8,128)} %get-tuple-element.14.rule_ref, bf16[27,128,128]{2,1,0:T(8,128)(2,1)} %w1_ref.3, bf16[768,128]{1,0:T(8,128)(2,1)} %grad_out_ref.3, s32[6]{0:T(128)} %live_ref.1), custom_call_target="tpu_custom_call" | custom-call | flops 5435817984 | bytes 1703960 | tf_op jit(solution)/shard_map/pallas_call | solution.py:271
  107.9 0.0 collective-permute-done.5
  107.9 2.1 %convert_multiply_fusion = (f32[3456,128]{1,0:T(8,128)}, f32[3456,128]{1,0:T(8,128)}) fusion(pred[]{:T(512)S(6)} %eq.4, bf16[3584,128]{1,0:T(8,128)(2,1)S(1)} %collective-permute-done.5, bf16[3584,128]{1,0:T(8,128)(2,1)S(1)} %bitcast.8), kind=kLoop, calls=%fused_computation.2 | loop fusion | flops 2654208 | bytes 5308417 | tf_op jit(solution)/shard_map/div | solution.py:341
  (2 shorter events, 0.0 us)
Async XLA Ops:
  2.8 8.1 %collective-permute-start = (bf16[320,256]{1,0:T(8,128)(2,1)}, bf16[320,256]{1,0:T(8,128)(2,1)S(1)}, u32[]{:S(2)}, u32[]{:S(2)}) collective-permute-start(bf16[320,256]{1,0:T(8,128)(2,1)} %get-tuple-element.11), channel_id=1, source_target_pairs={{0,1},{1,0},{2,3},{3,2},{4,5},{5,4},{6,7},{7,6},{8,9},{9,8},{10,11... | collective-permute-start | bytes 491528 | tf_op jit(solution)/shard_map/ppermute | solution.py:21
  4.8 6.1 %collective-permute-start.1 = (bf16[320,256]{1,0:T(8,128)(2,1)}, bf16[320,256]{1,0:T(8,128)(2,1)S(1)}, u32[]{:S(2)}, u32[]{:S(2)}) collective-permute-start(bf16[320,256]{1,0:T(8,128)(2,1)} %get-tuple-element.12), channel_id=1, source_target_pairs={{1,2},{2,1},{3,4},{4,3},{5,6},{6,5},{7,8},{8,7},{9,10},{10,9},{11,... | collective-permute-start | bytes 491528 | tf_op jit(solution)/shard_map/ppermute | solution.py:21
  10.9 0.7 copy-start
  10.9 0.7 copy-start.1
  32.9 3.8 %collective-permute-start.2 = (bf16[3584,128]{1,0:T(8,128)(2,1)}, bf16[3584,128]{1,0:T(8,128)(2,1)S(1)}, u32[]{:S(2)}, u32[]{:S(2)}) collective-permute-start(bf16[3584,128]{1,0:T(8,128)(2,1)} %get-tuple-element.16), channel_id=1, source_target_pairs={{0,64},{64,0},{1,65},{65,1},{2,66},{66,2},{3,67},{67,3},{4,68},{68... | collective-permute-start | bytes 2752520 | tf_op jit(solution)/shard_map/ppermute | solution.py:37
  65.7 4.5 %collective-permute-start.3 = (f32[112,128]{1,0:T(8,128)S(1)}, f32[112,128]{1,0:T(8,128)S(1)}, u32[]{:S(2)}, u32[]{:S(2)}) collective-permute-start(f32[112,128]{1,0:T(8,128)S(1)} %convert_reduce_fusion), channel_id=1, source_target_pairs={{0,8},{8,0},{16,24},{24,16},{1,9},{9,1},{17,25},{25,17},{2,10},{10... | collective-permute-start | bytes 172040 | tf_op jit(solution)/shard_map/ppermute | solution.py:43
  70.2 6.4 %collective-permute-start.4 = (f32[112,128]{1,0:T(8,128)S(1)}, f32[112,128]{1,0:T(8,128)S(1)}, u32[]{:S(2)}, u32[]{:S(2)}) collective-permute-start(f32[112,128]{1,0:T(8,128)S(1)} %add.10), channel_id=1, source_target_pairs={{0,24},{8,16},{16,8},{24,0},{1,25},{9,17},{17,9},{25,1},{2,26},{10... | collective-permute-start | bytes 172040 | tf_op jit(solution)/shard_map/ppermute | solution.py:43
  93.8 14.2 %collective-permute-start.5 = (bf16[3584,128]{1,0:T(8,128)(2,1)S(1)}, bf16[3584,128]{1,0:T(8,128)(2,1)S(1)}, u32[]{:S(2)}, u32[]{:S(2)}) collective-permute-start(bf16[3584,128]{1,0:T(8,128)(2,1)S(1)} %bitcast.7), channel_id=1, source_target_pairs={{0,64},{64,0},{1,65},{65,1},{2,66},{66,2},{3,67},{67,3},{4,68},{68... | collective-permute-start | bytes 2752520 | tf_op jit(solution)/shard_map/ppermute | solution.py:46

commit v4 on v2

--- a/solution.py
+++ b/solution.py
@@ -130,35 +130,59 @@
     return total + jnp.dot(w_ref[...], low_ref[:, :used], preferred_element_type=jnp.float32)
 
 
-def pack_kernel(feat_ref, grad_ref, rule_ref, odd_ref, own_ref, to_even_ref, to_odd_ref):
+def pack_rows(out_ref, feat_ref, grad_ref, rule_ref, start):
     rows, chans = feat_ref.shape
     offsets = rule_ref.shape[0]
-    own_ref[2 * chans :, :] = jnp.zeros((2 * CODE, rows), jnp.bfloat16)
-    for b in range(rows // BLOCK):
+    count = out_ref.shape[1]
+    out_ref[2 * chans :, :] = jnp.zeros((2 * CODE, count), jnp.bfloat16)
+    for b in range(count // BLOCK):
         at = slice(b * BLOCK, (b + 1) * BLOCK)
-        own_ref[:chans, at] = feat_ref[at, :].T
-        own_ref[chans : 2 * chans, at] = grad_ref[at, :].T
-    entries = rule_ref[...]
+        source = slice(start + b * BLOCK, start + (b + 1) * BLOCK)
+        out_ref[:chans, at] = feat_ref[source, :].T
+        out_ref[chans : 2 * chans, at] = grad_ref[source, :].T
+    entries = rule_ref[:, start : start + count]
     code = jnp.where(entries == rows + 2 * HALO, 0, entries + 1)
     coarse = lax.shift_right_logical(code, 5).astype(jnp.float32).astype(jnp.bfloat16)
     fine = (code & 31).astype(jnp.float32).astype(jnp.bfloat16)
-    own_ref[2 * chans : 2 * chans + offsets, :] = coarse
-    own_ref[2 * chans + CODE : 2 * chans + CODE + offsets, :] = fine
-    first, last = own_ref[:, :EDGE], own_ref[:, rows - EDGE :]
-    odd = odd_ref[0] == 1
-    to_even_ref[...] = jnp.where(odd, first, last)
-    to_odd_ref[...] = jnp.where(odd, last, first)
+    out_ref[2 * chans : 2 * chans + offsets, :] = coarse
+    out_ref[2 * chans + CODE : 2 * chans + CODE + offsets, :] = fine
+
+
+def edges_kernel(feat_ref, grad_ref, rule_ref, odd_ref, to_even_ref, to_odd_ref):
+    last = feat_ref.shape[0] - EDGE
+
+    @pl.when(odd_ref[0] == 1)
+    def _():
+        pack_rows(to_even_ref, feat_ref, grad_ref, rule_ref, 0)
+        pack_rows(to_odd_ref, feat_ref, grad_ref, rule_ref, last)
+
+    @pl.when(odd_ref[0] != 1)
+    def _():
+        pack_rows(to_even_ref, feat_ref, grad_ref, rule_ref, last)
+        pack_rows(to_odd_ref, feat_ref, grad_ref, rule_ref, 0)
+
+
+def own_kernel(feat_ref, grad_ref, rule_ref, own_ref):
+    pack_rows(own_ref, feat_ref, grad_ref, rule_ref, 0)
 
 
 def grads_kernel(
-    own_ref, even_ref, odd_ref, grad_out_ref, w1_ref, w2_ref, core_ref, parity_ref,
+    own_ref, even_ref, odd_ref, grad_out_hbm, w1_hbm, w2_hbm, core_ref, parity_ref,
     mine_ref, other_ref, source_ref, rule_ref,
     high_ref, low_ref, picked_ref, w_ref, before_ref, after_ref, ids_ref,
+    grad_out_ref, w1_ref, w2_ref, grad_out_sem, w1_sem, w2_sem,
 ):
     rows, chans = grad_out_ref.shape
     offsets = w1_ref.shape[0]
     flat = offsets * chans
     wide = rows + 2 * HALO
+    arriving = [
+        pltpu.make_async_copy(grad_out_hbm, grad_out_ref, grad_out_sem),
+        pltpu.make_async_copy(w1_hbm, w1_ref, w1_sem),
+        pltpu.make_async_copy(w2_hbm, w2_ref, w2_sem),
+    ]
+    for copy in arriving:
+        copy.start()
     fill_ids(ids_ref)
     mine_ref[flat:, :] = jnp.zeros((mine_ref.shape[0] - flat, chans), jnp.float32)
     other_ref[flat:, :] = jnp.zeros((other_ref.shape[0] - flat, chans), jnp.bfloat16)
@@ -187,6 +211,8 @@
         gather(k, at)
 
     over_offsets(offsets, chans, both, GROUP)
+    for copy in arriving:
+        copy.wait()
     side_by_side(w2_ref, w_ref, False)
     grad_act = through(w_ref, high_ref, low_ref, wide)
     side_by_side(w1_ref, w_ref, True)
@@ -238,17 +264,18 @@
         out_ref[at, :] = (live_ref[b].astype(jnp.float32) * added).astype(jnp.bfloat16)
 
 
-def call(kernel, outs, scratch, *args, scalars=0, flops=0):
+def call(kernel, outs, scratch, *args, scalars=0, held=0, flops=0):
     vmem = pl.BlockSpec(memory_space=pltpu.VMEM)
+    hbm = pl.BlockSpec(memory_space=pl.ANY)
     smem = pl.BlockSpec(memory_space=pltpu.SMEM)
     shapes = [jax.ShapeDtypeStruct(shape, dtype) for shape, dtype in outs]
     moved = sum(x.size * x.dtype.itemsize for x in (*args, *shapes))
     return pl.pallas_call(
         kernel,
         out_shape=shapes,
-        in_specs=[vmem] * (len(args) - scalars) + [smem] * scalars,
+        in_specs=[vmem] * (len(args) - scalars - held) + [hbm] * held + [smem] * scalars,
         out_specs=[vmem] * len(outs),
-        scratch_shapes=[pltpu.VMEM(shape, dtype) for shape, dtype in scratch],
+        scratch_shapes=[pltpu.VMEM(*kind) for kind in scratch] + [pltpu.SemaphoreType.DMA] * held,
         cost_estimate=pl.CostEstimate(flops=flops, bytes_accessed=moved, transcendentals=0),
     )(*args)
 
@@ -266,23 +293,16 @@
     tall = 2 * chans + 2 * CODE
     one_pass = 2 * offsets * rows * SPAN * SPAN
     parity = (lax.axis_index("x").astype(i32) & 1).reshape(1)
-    own, to_even, to_odd = call(
-        pack_kernel,
-        [((tall, rows), bf16), ((tall, EDGE), bf16), ((tall, EDGE), bf16)],
-        [],
-        features,
-        grad_out,
-        rulebook,
-        parity,
-        scalars=1,
-    )
+    edge = ((tall, EDGE), bf16)
+    to_even, to_odd = call(edges_kernel, [edge, edge], [], features, grad_out, rulebook, parity, scalars=1)
+    (own,) = call(own_kernel, [((tall, rows), bf16)], [], features, grad_out, rulebook)
+    even = swapped(to_even, BLOCKS, 0)
     odd = swapped(to_odd, BLOCKS, 1)
-    even = swapped(to_even, BLOCKS, 0)
     core = lax.axis_index("core").astype(i32).reshape(1)
     mine, other, grad_hidden, wide_rules = call(
         grads_kernel,
         [((padded, chans), f32), ((padded, chans), bf16), ((chans, wide), bf16), ((CODE, rows + 2 * EDGE), i32)],
-        [spread, spread, spread, beside, ((tall, EDGE), bf16), ((tall, EDGE), bf16), ids],
+        [spread, spread, spread, beside, edge, edge, ids, (grad_out.shape, bf16), (w1.shape, bf16), (w2.shape, bf16)],
         own,
         even,
         odd,
@@ -292,6 +312,7 @@
         core,
         parity,
         scalars=2,
+        held=3,
         flops=6 * one_pass,
     )
     (grad_in,) = call(

time: 111 us -> 111 us (level)
  waiting for transfers between devices: 8.28 us -> 6.26 us
    ppermute x2, waiting for transfers between devices: 2.31 us -> 0.3 us  [swapped(): return lax.ppermute(x, axis, [(i, j) for i, j in pairs if 0 <= j < length])]
    pallas_call x3 -> x4, Pallas kernels: 34 us -> 35.1 us  [call(): pl.pallas_call(kernel, out_shape=shapes, in_specs=[vmem] * (len(args) - s...]
  transfers between devices with their start and end apart: 6 -> 6, of which waited for: 4 -> 4; matrix products, arithmetic and copies ran while one was open for 0% -> 0% of each run, Pallas kernels for 8% -> 10%
where the time goes in v4:
time: 111 us; the launch traced here: 110 us
  blocking collectives  43.3 us (39%)
  Pallas kernels  35.1 us (32%)
  starting transfers between devices  20.2 us (18%)
  waiting for transfers between devices  6.26 us (6%)
  other arithmetic  4.02 us (4%)
    pallas_call x4, Pallas kernels, call(): pl.pallas_call(kernel, out_shape=shapes, in_specs=[vmem] * (len(args) - s...  35.1 us
    all_to_all x1, blocking collectives, reduce_everywhere(): parts = lax.all_to_all(parts, PLANE, 0, 0, tiled=True)  26.3 us
    all_to_all x1, blocking collectives, reduce_everywhere(): parts = lax.all_to_all(parts, PLANE, 0, 0, tiled=True).reshape(-1, lanes)  17 us
    ppermute x2, starting transfers between devices, reduce_everywhere(): lax.ppermute(own, 'z_hi', [(i, i ^ flip) for i in range(lax.axis_size('z_...  8.63 us
    ppermute x1, starting transfers between devices, reduce_everywhere(): other = lax.ppermute(parts, 'core', SWAP)  4.92 us
    ppermute x1, starting transfers between devices, reduce_everywhere(): own = own + lax.ppermute(other, 'core', SWAP).astype(jnp.float32)  3.98 us
    ppermute x2, waiting for transfers between devices, reduce_everywhere(): lax.ppermute(own, 'z_hi', [(i, i ^ flip) for i in range(lax.axis_size('z_...  3.65 us
    ppermute x2, starting transfers between devices, swapped(): return lax.ppermute(x, axis, [(i, j) for i, j in pairs if 0 <= j < length])  2.69 us
  transfers between devices with their start and end apart: 6, of which 4 were waited for; matrix products, arithmetic and copies ran while one was open for 0% of the time, Pallas kernels for 10%

profile of v4, /device:TPU:1, one launch (start us, length us, event | category | flops | bytes accessed | tf_op | source)
XLA Modules:
  0.0 110.4 jit_solution(13163601134080224402)
XLA Ops:
  0.6 1.9 %shard_map.86 = (bf16[320,256]{1,0:T(8,128)(2,1)}, bf16[320,256]{1,0:T(8,128)(2,1)}) custom-call(bf16[768,128]{1,0:T(8,128)(2,1)} %feat_ref.3, bf16[768,128]{1,0:T(8,128)(2,1)} %grad_out_ref.1, s32[27,768]{1,0:T(8,128)} %rule_ref.3, s32[1]{0:T(128)} %bitcast.odd_ref.parity_ref), custom_call_target="tpu_custom_call" | custom-call | bytes 803844 | tf_op jit(solution)/shard_map/pallas_call | solution.py:273
  2.6 2.0 %collective-permute-start = (bf16[320,256]{1,0:T(8,128)(2,1)}, bf16[320,256]{1,0:T(8,128)(2,1)S(1)}, u32[]{:S(2)}, u32[]{:S(2)}) collective-permute-start(bf16[320,256]{1,0:T(8,128)(2,1)} %get-tuple-element.9), channel_id=1, source_target_pairs={{0,1},{1,0},{2,3},{3,2},{4,5},{5,4},{6,7},{7,6},{8,9},{9,8},{10,11... | collective-permute-start | bytes 491528 | tf_op jit(solution)/shard_map/ppermute | solution.py:21
  4.6 0.7 collective-permute-start.1
  5.3 2.0 %shard_map.85.own_ref = bf16[320,768]{1,0:T(8,128)(2,1)} custom-call(bf16[768,128]{1,0:T(8,128)(2,1)} %feat_ref.3, bf16[768,128]{1,0:T(8,128)(2,1)} %grad_out_ref.1, s32[27,768]{1,0:T(8,128)} %rule_ref.3), custom_call_target="tpu_custom_call" | custom-call | bytes 967680 | tf_op jit(solution)/shard_map/pallas_call | solution.py:273
  7.3 0.3 collective-permute-done.even_ref
  7.6 0.0 copy-start
  7.6 0.0 collective-permute-done.1.odd_ref
  7.6 0.0 copy-start.1
  7.6 0.7 copy-done
  8.3 0.0 copy-done.1
  8.3 21.9 %shard_map.87 = (f32[3584,128]{1,0:T(8,128)}, bf16[3584,128]{1,0:T(8,128)(2,1)}, bf16[128,1024]{1,0:T(8,128)(2,1)}, s32[32,1280]{1,0:T(8,128)}) custom-call(bf16[320,768]{1,0:T(8,128)(2,1)} %shard_map.85.own_ref, bf16[320,256]{1,0:T(8,128)(2,1)} %copy-done, bf16[320,256]{1,0:T(8,128)(2,1)} %copy-done.1, bf16[768,128]{1,0:T(8,128)(2,1)} %grad_out_ref.1, ...), custom_call_target="tpu_custom_call" | custom-call | flops 16307453952 | bytes 5963784 | tf_op jit(solution)/shard_map/pallas_call | solution.py:273
  30.2 4.0 %collective-permute-start.2 = (bf16[3584,128]{1,0:T(8,128)(2,1)}, bf16[3584,128]{1,0:T(8,128)(2,1)S(1)}, u32[]{:S(2)}, u32[]{:S(2)}) collective-permute-start(bf16[3584,128]{1,0:T(8,128)(2,1)} %get-tuple-element.14), channel_id=1, source_target_pairs={{0,64},{64,0},{1,65},{65,1},{2,66},{66,2},{3,67},{67,3},{4,68},{68... | collective-permute-start | bytes 2752520 | tf_op jit(solution)/shard_map/ppermute | solution.py:37
  34.2 2.3 %collective-permute-done.2 = bf16[3584,128]{1,0:T(8,128)(2,1)S(1)} collective-permute-done((bf16[3584,128]{1,0:T(8,128)(2,1)}, bf16[3584,128]{1,0:T(8,128)(2,1)S(1)}, u32[]{:S(2)}, u32[]{:S(2)}) %collective-permute-start.2) | collective-permute-done | bytes 917536 | tf_op jit(solution)/shard_map/ppermute | solution.py:37
  36.5 1.7 %add_convert_fusion = bf16[3584,128]{1,0:T(8,128)(2,1)S(1)} fusion(f32[3584,128]{1,0:T(8,128)} %get-tuple-element.13, bf16[3584,128]{1,0:T(8,128)(2,1)S(1)} %collective-permute-done.2), kind=kLoop, calls=%fused_computation.1 | loop fusion | flops 1376256 | bytes 3670016 | tf_op jit(solution)/shard_map/convert_element_type | solution.py:39
  38.3 26.3 %all_to_all.10 = bf16[32,112,128]{2,1,0:T(8,128)(2,1)S(1)} all-to-all(bf16[32,112,128]{2,1,0:T(8,128)(2,1)S(1)} %bitcast.6), channel_id=1, replica_groups=mesh['yh'=2,'core'=2,'yl'=2,'z_hi'=4,'z_lo'=2,'x'=4] {'yh','yl','z_lo','x'}, dimensions={0} | all-to-all | bytes 1835008 | tf_op jit(solution)/shard_map/all_to_all | solution.py:40
  64.6 0.1 convert_reduce_fusion
  64.7 3.6 %collective-permute-start.3 = (f32[112,128]{1,0:T(8,128)S(1)}, f32[112,128]{1,0:T(8,128)S(1)}, u32[]{:S(2)}, u32[]{:S(2)}) collective-permute-start(f32[112,128]{1,0:T(8,128)S(1)} %convert_reduce_fusion), channel_id=1, source_target_pairs={{0,8},{8,0},{16,24},{24,16},{1,9},{9,1},{17,25},{25,17},{2,10},{10... | collective-permute-start | bytes 172040 | tf_op jit(solution)/shard_map/ppermute | solution.py:43
  68.4 2.0 %collective-permute-done.3 = f32[112,128]{1,0:T(8,128)S(1)} collective-permute-done((f32[112,128]{1,0:T(8,128)S(1)}, f32[112,128]{1,0:T(8,128)S(1)}, u32[]{:S(2)}, u32[]{:S(2)}) %collective-permute-start.3) | collective-permute-done | bytes 57376 | tf_op jit(solution)/shard_map/ppermute | solution.py:43
  70.4 5.0 %collective-permute-start.4 = (f32[112,128]{1,0:T(8,128)S(1)}, f32[112,128]{1,0:T(8,128)S(1)}, u32[]{:S(2)}, u32[]{:S(2)}) collective-permute-start(f32[112,128]{1,0:T(8,128)S(1)} %add.10), channel_id=1, source_target_pairs={{0,24},{8,16},{16,8},{24,0},{1,25},{9,17},{17,9},{25,1},{2,26},{10... | collective-permute-start | bytes 172040 | tf_op jit(solution)/shard_map/ppermute | solution.py:43
  75.4 1.6 %collective-permute-done.4 = f32[112,128]{1,0:T(8,128)S(1)} collective-permute-done((f32[112,128]{1,0:T(8,128)S(1)}, f32[112,128]{1,0:T(8,128)S(1)}, u32[]{:S(2)}, u32[]{:S(2)}) %collective-permute-start.4) | collective-permute-done | bytes 57376 | tf_op jit(solution)/shard_map/ppermute | solution.py:43
  77.0 0.1 broadcast_in_dim.2
  77.2 17.0 %all_to_all.11 = bf16[32,112,128]{2,1,0:T(8,128)(2,1)S(1)} all-to-all(bf16[32,112,128]{2,1,0:T(8,128)(2,1)S(1)} %broadcast_in_dim.2), channel_id=1, replica_groups=mesh['yh'=2,'core'=2,'yl'=2,'z_hi'=4,'z_lo'=2,'x'=4] {'yh','yl','z_lo','x'}, dimensions={0} | all-to-all | bytes 1835008 | tf_op jit(solution)/shard_map/all_to_all | solution.py:45
  94.1 4.9 %collective-permute-start.5 = (bf16[3584,128]{1,0:T(8,128)(2,1)S(1)}, bf16[3584,128]{1,0:T(8,128)(2,1)S(1)}, u32[]{:S(2)}, u32[]{:S(2)}) collective-permute-start(bf16[3584,128]{1,0:T(8,128)(2,1)S(1)} %bitcast.7), channel_id=1, source_target_pairs={{0,64},{64,0},{1,65},{65,1},{2,66},{66,2},{3,67},{67,3},{4,68},{68... | collective-permute-start | bytes 2752520 | tf_op jit(solution)/shard_map/ppermute | solution.py:46
  99.1 9.2 %shard_map.88 = bf16[768,128]{1,0:T(8,128)(2,1)} custom-call(bf16[128,1024]{1,0:T(8,128)(2,1)} %get-tuple-element.11.source_ref, s32[32,1280]{1,0:T(8,128)} %get-tuple-element.12.rule_ref, bf16[27,128,128]{2,1,0:T(8,128)(2,1)} %w1_ref.1, bf16[768,128]{1,0:T(8,128)(2,1)} %grad_out_ref.1, s32[6]{0:T(128)} %live_ref.1), custom_call_target="tpu_custom_call" | custom-call | flops 5435817984 | bytes 1703960 | tf_op jit(solution)/shard_map/pallas_call | solution.py:273
  108.3 0.0 collective-permute-done.5
  108.3 2.1 %convert_multiply_fusion = (f32[3456,128]{1,0:T(8,128)}, f32[3456,128]{1,0:T(8,128)}) fusion(pred[]{:T(512)S(6)} %eq.4, bf16[3584,128]{1,0:T(8,128)(2,1)S(1)} %collective-permute-done.5, bf16[3584,128]{1,0:T(8,128)(2,1)S(1)} %bitcast.8), kind=kLoop, calls=%fused_computation.2 | loop fusion | flops 2654208 | bytes 5308417 | tf_op jit(solution)/shard_map/div | solution.py:333
  (2 shorter events, 0.0 us)
Async XLA Ops:
  2.6 5.0 %collective-permute-start = (bf16[320,256]{1,0:T(8,128)(2,1)}, bf16[320,256]{1,0:T(8,128)(2,1)S(1)}, u32[]{:S(2)}, u32[]{:S(2)}) collective-permute-start(bf16[320,256]{1,0:T(8,128)(2,1)} %get-tuple-element.9), channel_id=1, source_target_pairs={{0,1},{1,0},{2,3},{3,2},{4,5},{5,4},{6,7},{7,6},{8,9},{9,8},{10,11... | collective-permute-start | bytes 491528 | tf_op jit(solution)/shard_map/ppermute | solution.py:21
  4.6 3.0 %collective-permute-start.1 = (bf16[320,256]{1,0:T(8,128)(2,1)}, bf16[320,256]{1,0:T(8,128)(2,1)S(1)}, u32[]{:S(2)}, u32[]{:S(2)}) collective-permute-start(bf16[320,256]{1,0:T(8,128)(2,1)} %get-tuple-element.10), channel_id=1, source_target_pairs={{1,2},{2,1},{3,4},{4,3},{5,6},{6,5},{7,8},{8,7},{9,10},{10,9},{11,... | collective-permute-start | bytes 491528 | tf_op jit(solution)/shard_map/ppermute | solution.py:21
  7.6 0.7 copy-start
  7.6 0.7 copy-start.1
  30.2 6.3 %collective-permute-start.2 = (bf16[3584,128]{1,0:T(8,128)(2,1)}, bf16[3584,128]{1,0:T(8,128)(2,1)S(1)}, u32[]{:S(2)}, u32[]{:S(2)}) collective-permute-start(bf16[3584,128]{1,0:T(8,128)(2,1)} %get-tuple-element.14), channel_id=1, source_target_pairs={{0,64},{64,0},{1,65},{65,1},{2,66},{66,2},{3,67},{67,3},{4,68},{68... | collective-permute-start | bytes 2752520 | tf_op jit(solution)/shard_map/ppermute | solution.py:37
  64.7 5.7 %collective-permute-start.3 = (f32[112,128]{1,0:T(8,128)S(1)}, f32[112,128]{1,0:T(8,128)S(1)}, u32[]{:S(2)}, u32[]{:S(2)}) collective-permute-start(f32[112,128]{1,0:T(8,128)S(1)} %convert_reduce_fusion), channel_id=1, source_target_pairs={{0,8},{8,0},{16,24},{24,16},{1,9},{9,1},{17,25},{25,17},{2,10},{10... | collective-permute-start | bytes 172040 | tf_op jit(solution)/shard_map/ppermute | solution.py:43
  70.4 6.6 %collective-permute-start.4 = (f32[112,128]{1,0:T(8,128)S(1)}, f32[112,128]{1,0:T(8,128)S(1)}, u32[]{:S(2)}, u32[]{:S(2)}) collective-permute-start(f32[112,128]{1,0:T(8,128)S(1)} %add.10), channel_id=1, source_target_pairs={{0,24},{8,16},{16,8},{24,0},{1,25},{9,17},{17,9},{25,1},{2,26},{10... | collective-permute-start | bytes 172040 | tf_op jit(solution)/shard_map/ppermute | solution.py:43
  94.1 14.2 %collective-permute-start.5 = (bf16[3584,128]{1,0:T(8,128)(2,1)S(1)}, bf16[3584,128]{1,0:T(8,128)(2,1)S(1)}, u32[]{:S(2)}, u32[]{:S(2)}) collective-permute-start(bf16[3584,128]{1,0:T(8,128)(2,1)S(1)} %bitcast.7), channel_id=1, source_target_pairs={{0,64},{64,0},{1,65},{65,1},{2,66},{66,2},{3,67},{67,3},{4,68},{68... | collective-permute-start | bytes 2752520 | tf_op jit(solution)/shard_map/ppermute | solution.py:46
